TPU v7x, 512 devices: a whole 4x8x8 slice. The times are simulated.
512 devices in a mesh: wide: 128 (over y_hi, x, z), narrow: 4 (over y_lo, core).
Axes of the slice: x: 4, y: 8 (y_hi: 4, y_lo: 2; y = y_hi * 2 + y_lo), z: 8, core: 2. Of those that a mesh axis runs over, the one named last changes fastest.
Arguments:
- tokens: bfloat16 [16384, 1024], P('wide'), may hold values from -6 to 6
- cotangent: bfloat16 [16384, 1024], P('wide'), may hold values from -6 to 6
- expert_ids: int32 [16384, 1], P('wide'), may hold values from 0 to 31; in each aligned block of 128 rows (0 to 127, 128 to 255, ...) at most 16 rows name the same one
- route_prob: float32 [16384], P('wide'), may hold values from 0.2 to 1
- gate_weight: bfloat16 [32768, 2816], P('wide', 'narrow'), may hold values from -0.1875 to 0.1875
- up_weight: bfloat16 [32768, 2816], P('wide', 'narrow'), may hold values from -0.1875 to 0.1875
- down_weight: bfloat16 [32768, 2816], P('wide', 'narrow'), may hold values from -0.109375 to 0.109375
Outputs:
- output: bfloat16 [16384, 1024], P('wide', 'narrow')
- tokens_grad: bfloat16 [16384, 1024], P('wide', 'narrow')
- prob_grad: float32 [16384], P('wide')
- gate_grad: float32 [32768, 2816], P('wide', 'narrow')
- up_grad: float32 [32768, 2816], P('wide', 'narrow')
- down_grad: float32 [32768, 2816], P('wide', 'narrow')
Inputs may be any that keep to these rules, and one draw needn't show every extreme that they name: `expert_ids`: among the 128 tokens of one index of wide, no expert is chosen by more than 16 tokens, and in some such groups one expert is chosen by exactly 16.
All inputs are finite; a program needn't handle non-finite values.
Results may differ from a plain program's by a relative error of at most 0.01.
Values may be sent and summed in bfloat16 or wider, within the bound.
A program may use at most 64 MiB of HBM per device.

v0:
```python
import jax
import jax.numpy as jnp
from jax import lax
from jax.sharding import PartitionSpec as P


def partner_2(x, axis, apart):
    return lax.ppermute(x, axis, [(i, i ^ 1 << apart) for i in range(lax.axis_size(axis))])


def transpose_dot(left, right):
    return lax.dot_general(
        left, right, (((1,), (1,)), ((), ())), preferred_element_type=jnp.float32
    )


def rows_dot(left, right):
    return lax.dot_general(
        left, right, (((0,), (0,)), ((), ())), preferred_element_type=jnp.float32
    )


def columns(array, first, count):
    return lax.dynamic_slice_in_dim(array, first, count, 1)


def shards(tokens, cotangent, expert_ids, route_prob, gate_weight, up_weight, down_weight):
    wide_count = lax.axis_size("wide")
    expert_count = wide_count // 4
    tok_rows, feature_width = tokens.shape
    hidden_width = gate_weight.shape[1]
    capacity = min(4 * tok_rows // expert_count, tok_rows)
    slot_count = capacity // 4
    total_rows = wide_count * slot_count
    block_rows = min(128, total_rows)
    member_index = lax.axis_index("wide") % 4
    low_bit = member_index % 2
    high_bit = member_index // 2
    chosen = expert_ids[:, 0]
    onehot = (chosen[:, None] == jnp.arange(expert_count, dtype=jnp.int32)[None, :]).astype(
        jnp.int32
    )
    token_rank = jnp.sum((jnp.cumsum(onehot, axis=0) - onehot) * onehot, axis=1)
    target = 4 * chosen + (token_rank + member_index) % 4
    slot_place = target * slot_count + token_rank // 4
    source = (
        jnp.full((total_rows,), tok_rows, jnp.int32)
        .at[slot_place]
        .set(jnp.arange(tok_rows, dtype=jnp.int32))
    )
    sent_counts = jnp.sum(
        (target[:, None] == jnp.arange(wide_count, dtype=jnp.int32)[None, :]).astype(jnp.int32),
        axis=0,
    )
    scaled = (route_prob[:, None] * cotangent.astype(jnp.float32)).astype(jnp.bfloat16)
    blank_row = jnp.zeros((1, feature_width), jnp.bfloat16)
    send_tokens = jnp.concatenate([tokens, blank_row], 0)[source]
    send_scaled = jnp.concatenate([scaled, blank_row], 0)[source]
    got_tokens, got_scaled, got_counts = (
        lax.all_to_all(send_tokens, "wide", split_axis=0, concat_axis=0, tiled=True),
        lax.all_to_all(send_scaled, "wide", split_axis=0, concat_axis=0, tiled=True),
        lax.all_to_all(
            sent_counts[:, None].astype(jnp.bfloat16),
            "wide",
            split_axis=0,
            concat_axis=0,
            tiled=True,
        ),
    )
    live_mask = (
        jnp.arange(slot_count, dtype=jnp.int32)[None, :] < got_counts.astype(jnp.int32)
    ).reshape(total_rows)
    live_rows = live_mask.astype(jnp.int32)
    filled = jnp.sum(live_rows)
    position = jnp.where(
        live_mask, jnp.cumsum(live_rows) - 1, filled + jnp.cumsum(1 - live_rows) - 1
    )
    packed_order = (
        jnp.zeros((total_rows,), jnp.int32)
        .at[position]
        .set(jnp.arange(total_rows, dtype=jnp.int32))
    )
    packed_tokens = got_tokens[packed_order]
    packed_scaled = got_scaled[packed_order]
    stacked = jnp.stack([gate_weight, up_weight, down_weight])
    partner = partner_2(stacked, "wide", 0)
    stacked = jnp.where(
        low_bit == 0, jnp.concatenate([stacked, partner], 1), jnp.concatenate([partner, stacked], 1)
    )
    partner = partner_2(stacked, "wide", 1)
    stacked = jnp.where(
        high_bit == 0,
        jnp.concatenate([stacked, partner], 1),
        jnp.concatenate([partner, stacked], 1),
    )
    gate_full = stacked[0]
    up_full = stacked[1]
    down_full = stacked[2]

    def block_step(block_index, state_tuple):
        row_start = block_index * block_rows
        rows_in = lax.dynamic_slice_in_dim(packed_tokens, row_start, block_rows, 0)
        rows_cot = lax.dynamic_slice_in_dim(packed_scaled, row_start, block_rows, 0)
        gate_val = jnp.dot(rows_in, gate_full, preferred_element_type=jnp.float32)
        up_val = jnp.dot(rows_in, up_full, preferred_element_type=jnp.float32)
        gate_sigma = jax.nn.sigmoid(gate_val)
        active = gate_val * gate_sigma
        hidden = (active * up_val).astype(jnp.bfloat16)
        out_part = transpose_dot(hidden, down_full)
        d_hidden = jnp.dot(rows_cot, down_full, preferred_element_type=jnp.float32)
        d_gate = (d_hidden * up_val * gate_sigma * (1.0 + gate_val * (1.0 - gate_sigma))).astype(
            jnp.bfloat16
        )
        d_up = (d_hidden * active).astype(jnp.bfloat16)
        in_part = transpose_dot(d_gate, gate_full) + transpose_dot(d_up, up_full)
        out_buffer = lax.dynamic_update_slice_in_dim(state_tuple[0], out_part, row_start, 0)
        in_buffer = lax.dynamic_update_slice_in_dim(state_tuple[1], in_part, row_start, 0)
        grad_state = tuple(
            (
                lax.dynamic_update_slice_in_dim(buffer_arr, value_arr, row_start, 0)
                for buffer_arr, value_arr in zip(state_tuple[2:], (d_gate, d_up, hidden))
            )
        )
        return (out_buffer, in_buffer) + grad_state

    zero_rows = jnp.zeros((total_rows, feature_width), jnp.float32)
    empty_rows = jnp.zeros((total_rows, hidden_width), jnp.bfloat16)
    count_blocks = (filled + block_rows - 1) // block_rows
    results = lax.fori_loop(
        0, count_blocks, block_step, (zero_rows, zero_rows, empty_rows, empty_rows, empty_rows)
    )
    out_received = results[0][position]
    in_received = results[1][position]
    ffn_sum, grad_sum = (
        lax.psum_scatter(
            out_received.astype(jnp.bfloat16), "narrow", scatter_dimension=1, tiled=True
        ).astype(jnp.float32),
        lax.psum_scatter(
            in_received.astype(jnp.bfloat16), "narrow", scatter_dimension=1, tiled=True
        ).astype(jnp.float32),
    )
    back_out, back_in = (
        lax.all_to_all(
            ffn_sum.astype(jnp.bfloat16), "wide", split_axis=0, concat_axis=0, tiled=True
        ),
        lax.all_to_all(
            grad_sum.astype(jnp.bfloat16), "wide", split_axis=0, concat_axis=0, tiled=True
        ),
    )
    ffn_tokens = back_out[slot_place]
    grad_tokens = back_in[slot_place]
    narrow_width = feature_width // lax.axis_size("narrow")
    cot_columns = columns(cotangent, lax.axis_index("narrow") * narrow_width, narrow_width).astype(
        jnp.float32
    )
    ffn_values = ffn_tokens.astype(jnp.float32)
    output = (route_prob[:, None] * ffn_values).astype(jnp.bfloat16)
    prob_grad = lax.psum(jnp.sum(ffn_values * cot_columns, axis=1), "narrow")
    half_width = feature_width // 2
    fourth = feature_width // 4
    full_grads = jnp.stack(
        [
            rows_dot(packed_tokens, results[2]),
            rows_dot(packed_tokens, results[3]),
            rows_dot(packed_scaled, results[4]),
        ]
    )
    kept = lax.dynamic_slice_in_dim(full_grads, high_bit * half_width, half_width, 1)
    kept = kept + partner_2(
        lax.dynamic_slice_in_dim(full_grads, (1 - high_bit) * half_width, half_width, 1).astype(
            jnp.bfloat16
        ),
        "wide",
        1,
    ).astype(jnp.float32)
    final = lax.dynamic_slice_in_dim(kept, low_bit * fourth, fourth, 1)
    final = final + partner_2(
        lax.dynamic_slice_in_dim(kept, (1 - low_bit) * fourth, fourth, 1).astype(jnp.bfloat16),
        "wide",
        0,
    ).astype(jnp.float32)
    gate_grad = final[0]
    up_grad = final[1]
    down_grad = final[2]
    return (output, grad_tokens, prob_grad, gate_grad, up_grad, down_grad)


def solution(mesh):
    in_specs = (
        P("wide", None),
        P("wide", None),
        P("wide", None),
        P("wide"),
        P("wide", "narrow"),
        P("wide", "narrow"),
        P("wide", "narrow"),
    )
    out_specs = (
        P("wide", "narrow"),
        P("wide", "narrow"),
        P("wide"),
        P("wide", "narrow"),
        P("wide", "narrow"),
        P("wide", "narrow"),
    )
    return jax.shard_map(shards, mesh=mesh, in_specs=in_specs, out_specs=out_specs, check_vma=False)
```

profile of v0, /device:TPU:1, one launch (start us, length us, event | category | flops | bytes accessed | tf_op | source)
XLA Modules:
  0.0 456.1 jit_solution(17685828918791412693)
XLA Ops:
  10.5 20.8 %all-to-all-start = ((bf16[128,1,1]{2,1,0:T(2,128)(2,1)}), bf16[128,1,1]{2,1,0:T(2,128)(2,1)S(1)}, u32[]{:S(2)}, u32[]{:S(2)}) async-start(bf16[128,1,1]{2,1,0:T(2,128)(2,1)} %copy.27), calls=%async_computation | async-start | bytes 131072 | tf_op jit(solution)/shard_map/all_to_all | solution.py:62
  36.7 7.2 %all-to-all-done = bf16[128,1,1]{2,1,0:T(2,128)(2,1)S(1)} async-done(((bf16[128,1,1]{2,1,0:T(2,128)(2,1)}), bf16[128,1,1]{2,1,0:T(2,128)(2,1)S(1)}, u32[]{:S(2)}, u32[]{:S(2)}) %all-to-all-start) | async-done | bytes 288 | tf_op jit(solution)/shard_map/all_to_all | solution.py:62
  43.8 9.2 %all-to-all-start.1 = ((bf16[128,4,1024]{2,1,0:T(4,128)(2,1)}), bf16[128,4,1024]{2,1,0:T(4,128)(2,1)}, u32[]{:S(2)}, u32[]{:S(2)}) async-start(bf16[128,4,1024]{2,1,0:T(4,128)(2,1)} %all_to_all.37), calls=%async_computation.1 | async-start | bytes 2097152 | tf_op jit(solution)/shard_map/all_to_all | solution.py:60
  53.1 2.4 collective-permute-start
  55.6 42.9 %collective-permute-done = bf16[3,256,704]{1,2,0:T(8,128)(2,1)} collective-permute-done((bf16[3,256,704]{1,2,0:T(8,128)(2,1)S(1)}, bf16[3,256,704]{1,2,0:T(8,128)(2,1)}, u32[]{:S(2)}, u32[]{:S(2)}) %collective-permute-start) | collective-permute-done | bytes 1081376 | tf_op jit(solution)/shard_map/ppermute | solution.py:8
  98.5 2.3 maximum_select_fusion.1
  100.9 4.7 %collective-permute-start.1 = (bf16[3,512,704]{1,2,0:T(8,128)(2,1)S(1)}, bf16[3,512,704]{1,2,0:T(8,128)(2,1)}, u32[]{:S(2)}, u32[]{:S(2)}) collective-permute-start(bf16[3,512,704]{1,2,0:T(8,128)(2,1)S(1)} %maximum_select_fusion.1), channel_id=1, source_target_pairs={{0,8},{4,12},{8,0},{12,4},{16,24},{20,28},{24,16},{28,20},{32,40},... | collective-permute-start | bytes 6488072 | tf_op jit(solution)/shard_map/ppermute | solution.py:8
  105.7 2.8 gather_fusion.2
  108.5 2.2 all_to_all.40
  110.8 14.0 %all-to-all-start.2 = ((bf16[128,4,1024]{2,1,0:T(4,128)(2,1)}), bf16[128,4,1024]{2,1,0:T(4,128)(2,1)}, u32[]{:S(2)}, u32[]{:S(2)}) async-start(bf16[128,4,1024]{2,1,0:T(4,128)(2,1)} %all_to_all.40), calls=%async_computation.2 | async-start | bytes 2097152 | tf_op jit(solution)/shard_map/all_to_all | solution.py:61
  125.1 2.4 convert_reduce_fusion
  131.3 2.4 scatter_custom_fusion.1
  135.1 2.8 gather_fusion.1
  137.9 86.8 %all-to-all-done.2 = bf16[128,4,1024]{2,1,0:T(4,128)(2,1)} async-done(((bf16[128,4,1024]{2,1,0:T(4,128)(2,1)}), bf16[128,4,1024]{2,1,0:T(4,128)(2,1)}, u32[]{:S(2)}, u32[]{:S(2)}) %all-to-all-start.2) | async-done | bytes 1048608 | tf_op jit(solution)/shard_map/all_to_all | solution.py:61
  226.1 2.8 gather_fusion.3
  228.8 3.0 maximum_select_fusion
  231.9 2.1 slice_bitcast_fusion
  236.4 2.6 copy.30
  243.9 18.2 %while.18 = (s32[]{:T(128)}, bf16[512,1024]{1,0:T(8,128)(2,1)}, bf16[512,1024]{1,0:T(8,128)(2,1)}, bf16[512,704]{0,1:T(8,128)(2,1)}, bf16[512,704]{0,1:T(8,128)(...) while((s32[]{:T(128)}, bf16[512,1024]{1,0:T(8,128)(2,1)}, ...), condition=%wide.region_11.12_spmd, body=%wide.region_10.11_spmd.sunk | while | flops 1108779008 | bytes 37406056 | solution.py:129
  247.4 2.6 constant_dynamic-update-slice_fusion.4
  256.5 2.6 constant_dynamic-update-slice_fusion.4
  262.1 5.0 %gather_fusion.4 = bf16[512,1024]{1,0:T(8,128)(2,1)} fusion(bf16[512,1024]{1,0:T(8,128)(2,1)} %get-tuple-element.73, s32[1024]{0:T(1024)S(1)} %pad_clamp_fusion.1), kind=kCustom, calls=%fused_computation.4 | custom fusion | bytes 2099200 | tf_op jit(solution)/shard_map/gather | solution.py:132
  271.9 3.3 copy-done.6
  277.5 2.8 gather_fusion.6
  280.3 25.4 %reduce-scatter.3.cloned.1.call-done = bf16[512,256]{1,0:T(8,128)(2,1)} async-done(((bf16[512,1024]{1,0:T(8,128)(2,1)}), bf16[512,256]{1,0:T(8,128)(2,1)}) %reduce-scatter.3.cloned.1.call-update) | async-done | bytes 262160 | tf_op jit(solution)/shard_map/reduce_scatter | solution.py:135
  307.4 15.9 %all-to-all-start.3 = ((bf16[128,4,256]{2,1,0:T(4,128)(2,1)}), bf16[128,4,256]{2,1,0:T(4,128)(2,1)S(1)}, u32[]{:S(2)}, u32[]{:S(2)}) async-start(bf16[128,4,256]{2,1,0:T(4,128)(2,1)} %all_to_all.43), calls=%async_computation.4 | async-start | bytes 524288 | tf_op jit(solution)/shard_map/all_to_all | solution.py:143
  323.3 54.9 %collective-permute-done.2 = bf16[3,512,704]{1,2,0:T(8,128)(2,1)} collective-permute-done((bf16[3,512,704]{1,2,0:T(8,128)(2,1)S(1)}, bf16[3,512,704]{1,2,0:T(8,128)(2,1)}, u32[]{:S(2)}, u32[]{:S(2)}) %collective-permute-start.2) | collective-permute-done | bytes 2162720 | tf_op jit(solution)/shard_map/ppermute | solution.py:8
  378.2 3.6 convert_add_fusion
  387.6 9.6 %all-to-all-done.3 = bf16[128,4,256]{2,1,0:T(4,128)(2,1)S(1)} async-done(((bf16[128,4,256]{2,1,0:T(4,128)(2,1)}), bf16[128,4,256]{2,1,0:T(4,128)(2,1)S(1)}, u32[]{:S(2)}, u32[]{:S(2)}) %all-to-all-start.3) | async-done | bytes 262176 | tf_op jit(solution)/shard_map/all_to_all | solution.py:143
  397.2 16.9 %all-to-all-start.4 = ((bf16[128,4,256]{2,1,0:T(4,128)(2,1)}), bf16[128,4,256]{2,1,0:T(4,128)(2,1)S(1)}, u32[]{:S(2)}, u32[]{:S(2)}) async-start(bf16[128,4,256]{2,1,0:T(4,128)(2,1)} %all_to_all.46), calls=%async_computation.6 | async-start | bytes 524288 | tf_op jit(solution)/shard_map/all_to_all | solution.py:146
  415.1 20.6 %all-to-all-done.4 = bf16[128,4,256]{2,1,0:T(4,128)(2,1)S(1)} async-done(((bf16[128,4,256]{2,1,0:T(4,128)(2,1)}), bf16[128,4,256]{2,1,0:T(4,128)(2,1)S(1)}, u32[]{:S(2)}, u32[]{:S(2)}) %all-to-all-start.4) | async-done | bytes 262176 | tf_op jit(solution)/shard_map/all_to_all | solution.py:146
  438.8 7.2 %psum.7 = f32[128]{0:T(128)} all-reduce(f32[128]{0:T(128)S(1)} %get-tuple-element.158), channel_id=1, replica_groups=mesh['wide'=128,'narrow'=4] {'narrow'}, use_global_device_ids=true, to_apply=%region_15.16 | all-reduce | flops 128 | bytes 1024 | tf_op jit(solution)/shard_map/psum | solution.py:158
  (145 shorter events, 56.9 us)
Async XLA Ops:
  9.6 22.7 %copy-start.23 = (s32[128]{0:T(128)}, s32[128]{0:T(128)S(1)}, u32[]{:S(2)}) copy-start(s32[128]{0:T(128)S(1)} %get-tuple-element.146) | copy-start | bytes 1540
  10.5 33.3 %all-to-all-start = ((bf16[128,1,1]{2,1,0:T(2,128)(2,1)}), bf16[128,1,1]{2,1,0:T(2,128)(2,1)S(1)}, u32[]{:S(2)}, u32[]{:S(2)}) async-start(bf16[128,1,1]{2,1,0:T(2,128)(2,1)} %copy.27), calls=%async_computation | async-start | bytes 131072 | tf_op jit(solution)/shard_map/all_to_all | solution.py:62
  35.4 17.6 %copy-start.9 = (bf16[256,704]{0,1:T(8,128)(2,1)S(1)}, bf16[256,704]{0,1:T(8,128)(2,1)}, u32[]{:S(2)}) copy-start(bf16[256,704]{0,1:T(8,128)(2,1)} %param.15) | copy-start | bytes 1081348
  35.4 17.6 %copy-start.11 = (bf16[256,704]{0,1:T(8,128)(2,1)S(1)}, bf16[256,704]{0,1:T(8,128)(2,1)}, u32[]{:S(2)}) copy-start(bf16[256,704]{0,1:T(8,128)(2,1)} %param.14) | copy-start | bytes 1081348
  35.4 17.6 %copy-start.13 = (bf16[256,704]{0,1:T(8,128)(2,1)S(1)}, bf16[256,704]{0,1:T(8,128)(2,1)}, u32[]{:S(2)}) copy-start(bf16[256,704]{0,1:T(8,128)(2,1)} %param.13) | copy-start | bytes 1081348
  36.6 61.9 %copy-start.10 = (bf16[256,704]{0,1:T(8,128)(2,1)S(1)}, bf16[256,704]{0,1:T(8,128)(2,1)}, u32[]{:S(2)}) copy-start(bf16[256,704]{0,1:T(8,128)(2,1)} %param.15) | copy-start | bytes 1081348
  36.7 61.9 %copy-start.12 = (bf16[256,704]{0,1:T(8,128)(2,1)S(1)}, bf16[256,704]{0,1:T(8,128)(2,1)}, u32[]{:S(2)}) copy-start(bf16[256,704]{0,1:T(8,128)(2,1)} %param.14) | copy-start | bytes 1081348
  43.8 66.9 %all-to-all-start.1 = ((bf16[128,4,1024]{2,1,0:T(4,128)(2,1)}), bf16[128,4,1024]{2,1,0:T(4,128)(2,1)}, u32[]{:S(2)}, u32[]{:S(2)}) async-start(bf16[128,4,1024]{2,1,0:T(4,128)(2,1)} %all_to_all.37), calls=%async_computation.1 | async-start | bytes 2097152 | tf_op jit(solution)/shard_map/all_to_all | solution.py:60
  53.1 45.4 %collective-permute-start = (bf16[3,256,704]{1,2,0:T(8,128)(2,1)S(1)}, bf16[3,256,704]{1,2,0:T(8,128)(2,1)}, u32[]{:S(2)}, u32[]{:S(2)}) collective-permute-start(bf16[3,256,704]{1,2,0:T(8,128)(2,1)S(1)} %pad_maximum_fusion.1), channel_id=1, source_target_pairs={{0,4},{4,0},{8,12},{12,8},{16,20},{20,16},{24,28},{28,24},{32,36},... | collective-permute-start | bytes 3244040 | tf_op jit(solution)/shard_map/ppermute | solution.py:8
  55.6 50.0 %copy-start.18 = (bf16[128,1024]{1,0:T(8,128)(2,1)S(1)}, bf16[128,1024]{1,0:T(8,128)(2,1)}, u32[]{:S(2)}) copy-start(bf16[128,1024]{1,0:T(8,128)(2,1)} %param.10) | copy-start | bytes 786436
  55.6 50.0 %copy-start.21 = (f32[128]{0:T(128)S(1)}, f32[128]{0:T(128)}, u32[]{:S(2)}) copy-start(f32[128]{0:T(128)} %param.12) | copy-start | bytes 1540
  55.6 50.1 %copy-start.20 = (s32[1024]{0:T(1024)S(1)}, s32[1024]{0:T(1024)}, u32[]{:S(2)}) copy-start(s32[1024]{0:T(1024)} %copy-done.19) | copy-start | bytes 12292
  100.9 128.0 %collective-permute-start.1 = (bf16[3,512,704]{1,2,0:T(8,128)(2,1)S(1)}, bf16[3,512,704]{1,2,0:T(8,128)(2,1)}, u32[]{:S(2)}, u32[]{:S(2)}) collective-permute-start(bf16[3,512,704]{1,2,0:T(8,128)(2,1)S(1)} %maximum_select_fusion.1), channel_id=1, source_target_pairs={{0,8},{4,12},{8,0},{12,4},{16,24},{20,28},{24,16},{28,20},{32,40},... | collective-permute-start | bytes 6488072 | tf_op jit(solution)/shard_map/ppermute | solution.py:8
  110.8 114.0 %all-to-all-start.2 = ((bf16[128,4,1024]{2,1,0:T(4,128)(2,1)}), bf16[128,4,1024]{2,1,0:T(4,128)(2,1)}, u32[]{:S(2)}, u32[]{:S(2)}) async-start(bf16[128,4,1024]{2,1,0:T(4,128)(2,1)} %all_to_all.40), calls=%async_computation.2 | async-start | bytes 2097152 | tf_op jit(solution)/shard_map/all_to_all | solution.py:61
  124.8 180.9 %reduce-scatter.3.cloned.1.call-start = ((), (), s32[]{:S(2)}) async-start(), calls=%async_computation.7 | async-start | bytes 1310720 | tf_op jit(solution)/shard_map/reduce_scatter | solution.py:135
  243.9 3.5 copy-start.5
  247.3 2.6 copy-start
  253.0 3.5 copy-start.5
  256.5 2.6 copy-start
  262.1 5.0 %copy-start.14 = (bf16[512,1024]{1,0:T(8,128)(2,1)S(1)}, bf16[512,1024]{1,0:T(8,128)(2,1)}, u32[]{:S(2)}) copy-start(bf16[512,1024]{1,0:T(8,128)(2,1)} %get-tuple-element.306) | copy-start | bytes 3145732
  262.1 5.0 %copy-start.17 = (bf16[512,704]{0,1:T(8,128)(2,1)S(1)}, bf16[512,704]{0,1:T(8,128)(2,1)}, u32[]{:S(2)}) copy-start(bf16[512,704]{0,1:T(8,128)(2,1)} %get-tuple-element.77) | copy-start | bytes 2162692
  267.1 118.8 %reduce-scatter.5.cloned.1.call-start = ((), (), s32[]{:S(2)}) async-start(), calls=%async_computation.8 | async-start | bytes 1310720 | tf_op jit(solution)/shard_map/reduce_scatter | solution.py:138
  267.2 1.4 copy-start.16
  271.9 3.3 copy-start.6
  275.2 2.3 copy-start.4
  275.5 102.6 %collective-permute-start.2 = (bf16[3,512,704]{1,2,0:T(8,128)(2,1)S(1)}, bf16[3,512,704]{1,2,0:T(8,128)(2,1)}, u32[]{:S(2)}, u32[]{:S(2)}) collective-permute-start(bf16[3,512,704]{1,2,0:T(8,128)(2,1)S(1)} %dynamic-slice_convert_fusion), channel_id=1, source_target_pairs={{0,8},{4,12},{8,0},{12,4},{16,24},{20,28},{24,16},{28,20},{32,40},... | collective-permute-start | bytes 6488072 | tf_op jit(solution)/shard_map/ppermute | solution.py:8
  307.4 89.8 %all-to-all-start.3 = ((bf16[128,4,256]{2,1,0:T(4,128)(2,1)}), bf16[128,4,256]{2,1,0:T(4,128)(2,1)S(1)}, u32[]{:S(2)}, u32[]{:S(2)}) async-start(bf16[128,4,256]{2,1,0:T(4,128)(2,1)} %all_to_all.43), calls=%async_computation.4 | async-start | bytes 524288 | tf_op jit(solution)/shard_map/all_to_all | solution.py:143
  381.8 2.0 copy-start.7
  383.8 30.4 %copy-start.24 = (s32[128]{0:T(128)S(1)}, s32[128]{0:T(128)}, u32[]{:S(2)}) copy-start(s32[128]{0:T(128)} %copy-done.23) | copy-start | bytes 1540
  383.9 53.3 %copy-start.22 = (f32[128]{0:T(128)S(1)}, f32[128]{0:T(128)}, u32[]{:S(2)}) copy-start(f32[128]{0:T(128)} %param.12) | copy-start | bytes 1540
  383.9 62.1 %collective-permute-start.3 = (bf16[3,256,704]{1,2,0:T(8,128)(2,1)S(1)}, bf16[3,256,704]{1,2,0:T(8,128)(2,1)S(1)}, u32[]{:S(2)}, u32[]{:S(2)}) collective-permute-start(bf16[3,256,704]{1,2,0:T(8,128)(2,1)S(1)} %dynamic-slice_convert_fusion.1), channel_id=1, source_target_pairs={{0,4},{4,0},{8,12},{12,8},{16,20},{20,16},{24,28},{28,24},{32,36},... | collective-permute-start | bytes 3244040 | tf_op jit(solution)/shard_map/ppermute | solution.py:8
  397.2 38.5 %all-to-all-start.4 = ((bf16[128,4,256]{2,1,0:T(4,128)(2,1)}), bf16[128,4,256]{2,1,0:T(4,128)(2,1)S(1)}, u32[]{:S(2)}, u32[]{:S(2)}) async-start(bf16[128,4,256]{2,1,0:T(4,128)(2,1)} %all_to_all.46), calls=%async_computation.6 | async-start | bytes 524288 | tf_op jit(solution)/shard_map/all_to_all | solution.py:146
  (9 other events, 10.7 us)
Sparse Core Ops, SparseCore 0:
  267.2 38.4 reduce-scatter.2
  308.5 31.6 reduce-scatter.4
where the time goes:
time: 457 us; the launch traced here: 456 us
  waiting for transfers between devices  247 us (54%)
  starting transfers between devices  88 us (19%)
  local copies, waits for them, and re-layouts  58.1 us (13%)
  other arithmetic  21.1 us (5%)
  matrix products  18.8 us (4%)
  between operations  15.4 us (3%)
  blocking collectives  7.18 us (2%)
    ppermute x4, waiting for transfers between devices, partner_2(): lax.ppermute(x, axis, [(i, i ^ 1 << apart) for i in range(lax.axis_size(a...  97.8 us
    all_to_all x1, waiting for transfers between devices, shards(): lax.all_to_all(send_scaled, 'wide', split_axis=0, concat_axis=0, tiled=True)  86.8 us
    reduce_scatter x1, waiting for transfers between devices, shards(): lax.psum_scatter(out_received.astype(jnp.bfloat16), 'narrow', scatter_dim...  25.4 us
    all_to_all x1, starting transfers between devices, shards(): lax.all_to_all(sent_counts[:, None].astype(jnp.bfloat16), 'wide', split_a...  20.8 us
    all_to_all x1, waiting for transfers between devices, shards(): lax.all_to_all(grad_sum.astype(jnp.bfloat16), 'wide', split_axis=0, conca...  20.6 us
    all_to_all x1, starting transfers between devices, shards(): lax.all_to_all(grad_sum.astype(jnp.bfloat16), 'wide', split_axis=0, conca...  16.9 us
    all_to_all x1, starting transfers between devices, shards(): lax.all_to_all(ffn_sum.astype(jnp.bfloat16), 'wide', split_axis=0, concat...  15.9 us
    all_to_all x1, starting transfers between devices, shards(): lax.all_to_all(send_scaled, 'wide', split_axis=0, concat_axis=0, tiled=True)  14 us
  transfers between devices with their start and end apart: 11, of which 7 were waited for; matrix products, arithmetic and copies ran while one was open for 8% of the time, Pallas kernels for 0%

commit v1 on v0

v1 whole, which is shorter than its diff:
```python
import functools

import jax
import jax.numpy as jnp
from jax import lax
from jax.experimental import pallas as pl
from jax.experimental.pallas import tpu as pltpu
from jax.sharding import PartitionSpec as P

CAP = 16
CHUNK = 256
F32 = jnp.float32
BF16 = jnp.bfloat16


def dot(a, b):
    return lax.dot_general(a, b, (((1,), (0,)), ((), ())), preferred_element_type=F32)


def dot_t(a, b):
    return lax.dot_general(a, b, (((1,), (1,)), ((), ())), preferred_element_type=F32)


def kernel(
    tok, cot, ids, prob, wg, wu, wd,
    o_out, o_grad, o_prob, o_gg, o_gu, o_gd,
    wall, sendbuf, x4, xt, pre, act3, out_acc, in_acc, gloc, r_right, r_left, stage,
    t1s, t1r, t2s, t2r, fo, back, place, probs, parts,
    ag_send, ag_recv, rs_send, rs_recv, a_send, a_recv, l_sem, n_send, n_recv,
    t1_send, t1_recv, t2_send, t2_recv, b_send, b_recv, p_send, p_recv,
):
    toks, width = tok.shape
    ff = wg.shape[1]
    nf, _, _, quarter, chunk = wall.shape
    experts = sendbuf.shape[0] // CAP
    rows = x4.shape[1]
    blocks = rows // CAP
    me = lax.axis_index("wide")
    n = lax.axis_index("narrow")
    m = lax.rem(me, 4)
    e0 = lax.div(me, 4)
    half = lax.rem(e0, 2)
    group = lax.div(me, 8)
    i0 = group * 2
    core_peer = n + 1 - 2 * lax.rem(n, 2)
    row_peer = lax.rem(n + 2, 4)
    far_peer = 3 - n

    def dest_of(e):
        h = lax.rem(e + half, 2)
        return 4 * e + m + h * (3 - 2 * m), i0 + h

    def source_of(i):
        h = lax.rem(i, 2)
        return lax.div(i, 2) * 8 + lax.rem(half + h, 2) * 4 + m + h * (3 - 2 * m)

    def remote(src, dst, ssem, rsem, wide, narrow):
        return pltpu.make_async_remote_copy(
            src_ref=src, dst_ref=dst, send_sem=ssem, recv_sem=rsem,
            device_id={"wide": wide, "narrow": narrow}, device_id_type=pl.DeviceIdType.MESH,
        )

    def await_bytes(ref, sem):
        pltpu.make_async_copy(ref, ref, sem).wait()

    for f in range(nf):
        w = min(chunk, ff - f * chunk)
        for k, ref in enumerate((wg, wu, wd)):
            part = ref[:, f * chunk : f * chunk + w]
            if w < chunk:
                part = jnp.concatenate([part, jnp.zeros((quarter, chunk - w), BF16)], axis=1)
            wall[f, m, k] = part

    barrier = pltpu.get_barrier_semaphore()

    def signal(wide, narrow):
        pl.semaphore_signal(
            barrier, inc=1, device_id={"wide": wide, "narrow": narrow},
            device_id_type=pl.DeviceIdType.MESH,
        )

    for turn in (1, 3):
        signal(4 * e0 + lax.rem(m + turn, 4), n)

    for peer in (core_peer, row_peer, far_peer):
        signal(me, peer)

    @pl.loop(1, experts)
    def _(j):
        signal(dest_of(lax.rem(e0 + j, experts))[0], n)

    @pl.loop(1, blocks)
    def _(j):
        signal(source_of(lax.rem(i0 + j, blocks)), n)

    def iota(shape, axis):
        return lax.broadcasted_iota(jnp.int32, shape, axis).astype(F32)

    slots = experts * CAP
    idf = ids[...].astype(F32)
    onehot = jnp.where(iota((toks, experts), 1) == idf, 1.0, 0.0)
    row_i, col_i = iota((toks, toks), 0), iota((toks, toks), 1)
    lower = jnp.where(col_i < row_i, 1.0, 0.0).astype(BF16)
    rank = jnp.sum(dot(lower, onehot.astype(BF16)) * onehot, axis=1, keepdims=True)
    slot = idf * CAP + rank
    place[...] = jnp.where(iota((toks, slots), 1) == slot, 1.0, 0.0).astype(BF16)
    diag = row_i == col_i
    slot_row = jnp.sum(jnp.where(diag, slot, 0.0), axis=0, keepdims=True)
    prob_col = jnp.sum(jnp.where(diag, prob[...], 0.0), axis=1, keepdims=True)
    probs[...] = jnp.broadcast_to(prob_col, (toks, quarter))
    columns = pl.ds(pl.multiple_of(n * quarter, quarter), quarter)
    pick = jnp.where(iota((slots, toks), 0) == slot_row, 1.0, 0.0).astype(BF16)
    scaled = (prob_col * cot[:, columns].astype(F32)).astype(BF16)
    sendbuf[:, :quarter] = dot(pick, tok[:, columns]).astype(BF16)
    sendbuf[:, quarter:] = dot(pick, scaled).astype(BF16)

    pl.semaphore_wait(barrier, experts - 1 + blocks - 1 + 5)

    def rows_at(i):
        return pl.ds(pl.multiple_of(i * CAP, CAP), CAP)

    local_in = pltpu.make_async_copy(
        sendbuf.at[rows_at(e0)], x4.at[n, rows_at(i0)], l_sem.at[0]
    )
    local_in.start()

    @pl.loop(1, experts)
    def _(j):
        e = lax.rem(e0 + j, experts)
        wide, block = dest_of(e)
        remote(sendbuf.at[rows_at(e)], x4.at[n, rows_at(block)], a_send, a_recv, wide, n).start()

    def ag_right(f, q):
        return remote(
            wall.at[f, q], wall.at[f, q], ag_send.at[0, f, q], ag_recv.at[f, q], me + 1, n
        )

    def ag_left(f, q):
        return remote(
            wall.at[f, q], wall.at[f, q], ag_send.at[1, f, q], ag_recv.at[f, q], me - 1, n
        )

    def ag_own(f):
        @pl.when(m < 3)
        def _():
            ag_right(f, m).start()

        @pl.when(m > 0)
        def _():
            ag_left(f, m).start()

    def ag_step(f, d):
        @pl.when(m >= d)
        def _():
            await_bytes(wall.at[f, m - d], ag_recv.at[f, m - d])

            @pl.when(m < 3)
            def _():
                ag_right(f, m - d).start()

        @pl.when(m + d <= 3)
        def _():
            await_bytes(wall.at[f, m + d], ag_recv.at[f, m + d])

            @pl.when(m > 0)
            def _():
                ag_left(f, m + d).start()

    ag_own(0)
    ag_step(0, 1)
    local_in.wait()
    await_bytes(x4.at[n, pl.ds(0, rows - CAP)], a_recv)
    to_row = remote(x4.at[n], x4.at[n], n_send.at[1], n_recv.at[n], me, row_peer)
    to_core = remote(x4.at[n], x4.at[n], n_send.at[0], n_recv.at[n], me, core_peer)
    to_row.start()
    to_core.start()
    out_acc[...] = jnp.zeros_like(out_acc)
    in_acc[...] = jnp.zeros_like(in_acc)
    ag_step(0, 2)
    await_bytes(x4.at[row_peer], n_recv.at[row_peer])
    relay = remote(x4.at[row_peer], x4.at[row_peer], n_send.at[2], n_recv.at[row_peer], me, core_peer)
    relay.start()
    ag_step(0, 3)
    ag_own(1)
    await_bytes(x4.at[core_peer], n_recv.at[core_peer])
    await_bytes(x4.at[far_peer], n_recv.at[far_peer])

    eye = jnp.where(iota((quarter, quarter), 0) == iota((quarter, quarter), 1), 1.0, 0.0).astype(BF16)

    @pl.loop(0, 4)
    def _(q):
        for k in range(2):
            part = pl.ds(k * quarter, quarter)
            xt[q, part, :] = dot_t(eye, x4[q, :, part]).astype(BF16)

    def rs_right(f, q):
        return remote(
            stage.at[f, q], r_right.at[f, q], rs_send.at[f, q], rs_recv.at[0, f, q], me + 1, n
        )

    def rs_left(f, q):
        return remote(
            stage.at[f, q], r_left.at[f, q], rs_send.at[f, q], rs_recv.at[1, f, q], me - 1, n
        )

    def rs_first(f):
        @pl.when(m == 0)
        def _():
            for q in (3, 2, 1):
                stage[f, q] = gloc[f, q].astype(BF16)
                rs_right(f, q).start()

        @pl.when(m == 3)
        def _():
            for q in (0, 1, 2):
                stage[f, q] = gloc[f, q].astype(BF16)
                rs_left(f, q).start()

    def rs_relay(f):
        for q, p in ((3, 0), (2, 1)):
            @pl.when((m > 0) & (m < q))
            def _():
                await_bytes(r_right.at[f, q], rs_recv.at[0, f, q])
                stage[f, q] = (gloc[f, q] + r_right[f, q].astype(F32)).astype(BF16)
                rs_right(f, q).start()

            @pl.when((m < 3) & (m > p))
            def _():
                await_bytes(r_left.at[f, p], rs_recv.at[1, f, p])
                stage[f, p] = (gloc[f, p] + r_left[f, p].astype(F32)).astype(BF16)
                rs_left(f, p).start()

    step_rows = min(64, rows)

    @pl.loop(0, nf)
    def _(f):
        for k, first, source in ((0, 0, 0), (1, 0, 1), (2, quarter, 2)):
            total = dot(x4[0, :, first : first + quarter], wall[f, 0, source])
            for q in range(1, 4):
                total += dot(x4[q, :, first : first + quarter], wall[f, q, source])
            pre[k] = total

        @pl.loop(0, rows // step_rows)
        def _(r):
            part = pl.ds(pl.multiple_of(r * step_rows, step_rows), step_rows)
            gate, up, d_hidden = pre[0, part], pre[1, part], pre[2, part]
            sigma = jax.nn.sigmoid(gate)
            active = gate * sigma
            act3[0, part] = (active * up).astype(BF16)
            act3[1, part] = (d_hidden * up * sigma * (1.0 + gate * (1.0 - sigma))).astype(BF16)
            act3[2, part] = (d_hidden * active).astype(BF16)

        @pl.loop(0, 4)
        def _(q):
            gloc[f, q, 0] = dot(xt[q, :quarter], act3[1])
            gloc[f, q, 1] = dot(xt[q, :quarter], act3[2])
            gloc[f, q, 2] = dot(xt[q, quarter:], act3[0])

        rs_first(f)

        @pl.loop(0, 4)
        def _(q):
            out_acc[q] += dot_t(act3[0], wall[f, q, 2])
            in_acc[q] += dot_t(act3[1], wall[f, q, 0]) + dot_t(act3[2], wall[f, q, 1])

        @pl.when(f + 1 < nf)
        def _():
            for d in (1, 2, 3):
                ag_step(f + 1, d)

            @pl.when(f + 2 < nf)
            def _():
                ag_own(f + 2)

        @pl.when(f >= 1)
        def _():
            rs_relay(f - 1)

    def both(q):
        return jnp.concatenate([out_acc[q], in_acc[q]], axis=1)

    t1s[1] = both(far_peer).astype(BF16)
    t1_far = remote(t1s.at[1], t1r.at[1], t1_send.at[1], t1_recv.at[1], me, core_peer)
    t1_far.start()
    t1s[0] = both(core_peer).astype(BF16)
    t1_near = remote(t1s.at[0], t1r.at[0], t1_send.at[0], t1_recv.at[0], me, core_peer)
    t1_near.start()
    t1_far.wait_recv()
    t2s[...] = (both(row_peer) + t1r[1].astype(F32)).astype(BF16)
    t2 = remote(t2s, t2r, t2_send, t2_recv, me, row_peer)
    t2.start()
    t1_near.wait_recv()
    t2.wait_recv()
    fo[...] = (both(n) + t1r[0].astype(F32) + t2r[...].astype(F32)).astype(BF16)

    local_back = pltpu.make_async_copy(fo.at[rows_at(i0)], back.at[rows_at(e0)], l_sem.at[1])
    local_back.start()

    @pl.loop(1, blocks)
    def _(j):
        i = lax.rem(i0 + j, blocks)
        remote(fo.at[rows_at(i)], back.at[rows_at(e0)], b_send, b_recv, source_of(i), n).start()

    rs_relay(nf - 1)

    def finish(f):
        w = min(chunk, ff - f * chunk)

        @pl.when(m > 0)
        def _():
            await_bytes(r_right.at[f, m], rs_recv.at[0, f, m])
            gloc[f, m] += r_right[f, m].astype(F32)

        @pl.when(m < 3)
        def _():
            await_bytes(r_left.at[f, m], rs_recv.at[1, f, m])
            gloc[f, m] += r_left[f, m].astype(F32)

        for k, ref in enumerate((o_gg, o_gu, o_gd)):
            ref[:, f * chunk : f * chunk + w] = gloc[f, m, k][:, :w]

    for f in range(nf - 1):
        finish(f)

    local_back.wait()
    await_bytes(back.at[pl.ds(0, slots - CAP)], b_recv)
    ffn = dot(place[...], back[:, :quarter])
    o_out[...] = (probs[...] * ffn).astype(BF16)
    o_grad[...] = dot(place[...], back[:, quarter:]).astype(BF16)
    part_col = jnp.sum(ffn * cot[:, columns].astype(F32), axis=1, keepdims=True)
    part_row = jnp.sum(jnp.where(diag, part_col, 0.0), axis=0, keepdims=True)
    parts[n] = jnp.broadcast_to(part_row, parts.shape[1:])
    sent = []
    for k, peer in enumerate((core_peer, row_peer, far_peer)):
        copy = remote(parts.at[n], parts.at[n], p_send.at[k], p_recv.at[n], me, peer)
        copy.start()
        sent.append(copy)
    finish(nf - 1)
    for peer in (core_peer, row_peer, far_peer):
        await_bytes(parts.at[peer], p_recv.at[peer])
    o_prob[...] = (parts[0] + parts[1] + parts[2] + parts[3])[:1]

    for copy in (*sent, to_row, to_core, relay, t1_near, t1_far, t2):
        copy.wait_send()
    await_bytes(sendbuf.at[pl.ds(0, slots - CAP)], a_send)
    await_bytes(fo.at[pl.ds(0, rows - CAP)], b_send)

    @pl.loop(0, nf)
    def _(f):
        for q in range(4):
            @pl.when(m != q)
            def _():
                await_bytes(stage.at[f, q], rs_send.at[f, q])

            @pl.when((m < 3) & (m >= q))
            def _():
                await_bytes(wall.at[f, q], ag_send.at[0, f, q])

            @pl.when((m > 0) & (m <= q))
            def _():
                await_bytes(wall.at[f, q], ag_send.at[1, f, q])


def shards(wide, tokens, cotangent, expert_ids, route_prob, gate_weight, up_weight, down_weight):
    toks, width = tokens.shape
    quarter, ff = gate_weight.shape
    experts = wide // 4
    slots = experts * CAP
    rows = wide // 4 * CAP
    chunk = min(CHUNK, quarter)
    nf = -(-ff // chunk)
    vmem, dma = pltpu.VMEM, pltpu.SemaphoreType.DMA
    spec = pl.BlockSpec(memory_space=pltpu.VMEM)
    grad = jax.ShapeDtypeStruct((quarter, ff), F32)
    two = 2 * quarter
    outs = pl.pallas_call(
        kernel,
        out_shape=(
            jax.ShapeDtypeStruct((toks, quarter), BF16),
            jax.ShapeDtypeStruct((toks, quarter), BF16),
            jax.ShapeDtypeStruct((1, toks), F32),
            grad, grad, grad,
        ),
        in_specs=[spec] * 7,
        out_specs=(spec,) * 6,
        scratch_shapes=[
            vmem((nf, 4, 3, quarter, chunk), BF16),
            vmem((slots, two), BF16),
            vmem((4, rows, two), BF16),
            vmem((4, two, rows), BF16),
            vmem((3, rows, chunk), F32),
            vmem((3, rows, chunk), BF16),
            vmem((4, rows, quarter), F32),
            vmem((4, rows, quarter), F32),
            vmem((nf, 4, 3, quarter, chunk), F32),
            vmem((nf, 4, 3, quarter, chunk), BF16),
            vmem((nf, 4, 3, quarter, chunk), BF16),
            vmem((nf, 4, 3, quarter, chunk), BF16),
            vmem((2, rows, two), BF16),
            vmem((2, rows, two), BF16),
            vmem((rows, two), BF16),
            vmem((rows, two), BF16),
            vmem((rows, two), BF16),
            vmem((slots, two), BF16),
            vmem((toks, slots), BF16),
            vmem((toks, quarter), F32),
            vmem((4, 8, toks), F32),
            dma((2, nf, 4)), dma((nf, 4)), dma((nf, 4)), dma((2, nf, 4)),
            dma, dma, dma((2,)), dma((3,)), dma((4,)),
            dma((2,)), dma((2,)), dma, dma, dma, dma, dma((3,)), dma((4,)),
        ],
        compiler_params=pltpu.CompilerParams(
            collective_id=0, has_side_effects=True, vmem_limit_bytes=63000 * 1024
        ),
    )(
        tokens, cotangent, expert_ids, route_prob.reshape(1, toks),
        gate_weight, up_weight, down_weight,
    )
    return outs[0], outs[1], outs[2].reshape(toks), outs[3], outs[4], outs[5]


def solution(mesh):
    in_specs = (
        P("wide", None),
        P("wide", None),
        P("wide", None),
        P("wide"),
        P("wide", "narrow"),
        P("wide", "narrow"),
        P("wide", "narrow"),
    )
    out_specs = (
        P("wide", "narrow"),
        P("wide", "narrow"),
        P("wide"),
        P("wide", "narrow"),
        P("wide", "narrow"),
        P("wide", "narrow"),
    )
    return jax.shard_map(
        functools.partial(shards, mesh.shape["wide"]),
        mesh=mesh, in_specs=in_specs, out_specs=out_specs, check_vma=False,
    )
```

time: 457 us -> 206 us (0.45)
  waiting for transfers between devices: 247 us -> 0 us
  Pallas kernels: 0 us -> 190 us
  starting transfers between devices: 88 us -> 0 us
  local copies, waits for them, and re-layouts: 58.1 us -> 11.9 us
  other arithmetic: 21.1 us -> 0 us
  matrix products: 18.8 us -> 0 us
  between operations: 15.4 us -> 0.67 us
  blocking collectives: 7.18 us -> 0 us
    pallas_call x0 -> x1, Pallas kernels: none -> 190 us  [shards(): pl.pallas_call(kernel, out_shape=(jax.ShapeDtypeStruct((toks, quarter), B...]
    all_to_all x5 -> x0, waiting for transfers between devices: 124 us -> none  [the longest x1 86.8 us: shards(): lax.all_to_all(send_scaled, 'wide', split_axis=0, concat_axis=0, tiled=True)]
    ppermute x4 -> x0, waiting for transfers between devices: 97.8 us -> none  [partner_2(): lax.ppermute(x, axis, [(i, i ^ 1 << apart) for i in range(lax.axis_size(a...]
    all_to_all x5 -> x0, starting transfers between devices: 76.7 us -> none  [the longest x1 20.8 us: shards(): lax.all_to_all(sent_counts[:, None].astype(jnp.bfloat16), 'wide', split_a...]
    reduce_scatter x2 -> x0, waiting for transfers between devices: 25.4 us -> none  [the longest x1 25.4 us: shards(): lax.psum_scatter(out_received.astype(jnp.bfloat16), 'narrow', scatter_dim...]
    gather x8 -> x0, local copies, waits for them, and re-layouts: 20.5 us -> none  [the longest x1 4.96 us: shards(): out_received = results[0][position]]
    dot_general x15 -> x0, matrix products: 18.8 us -> none  [the longest x2 5.21 us: block_step(): d_hidden = jnp.dot(rows_cot, down_full, preferred_element_type=jnp.float32)]
    ppermute x4 -> x0, starting transfers between devices: 10.9 us -> none  [partner_2(): lax.ppermute(x, axis, [(i, i ^ 1 << apart) for i in range(lax.axis_size(a...]
  transfers between devices with their start and end apart: 11 -> 0, of which waited for: 7 -> 0; matrix products, arithmetic and copies ran while one was open for 8% -> 0% of each run, Pallas kernels for 0% -> 0%
where the time goes in v1:
time: 206 us; the launch traced here: 203 us
  Pallas kernels  190 us (92%)
  local copies, waits for them, and re-layouts  11.9 us (6%)
    pallas_call x1, Pallas kernels, shards(): pl.pallas_call(kernel, out_shape=(jax.ShapeDtypeStruct((toks, quarter), B...  190 us
    unnamed x26, local copies, waits for them, and re-layouts  11.9 us

profile of v1, /device:TPU:1, one launch (start us, length us, event | category | flops | bytes accessed | tf_op | source)
XLA Modules:
  0.0 202.8 jit_solution(8266960093107148855)
XLA Ops:
  0.6 0.0 copy-start.6
  0.6 0.6 copy-done.6
  1.3 0.7 copy.13.ids
  2.0 0.0 copy-start.2
  2.0 2.0 copy.14.wg
  4.0 0.0 copy-done.2
  4.0 0.0 copy-start.3
  4.0 0.9 copy.15.wu
  4.9 0.1 copy-done.3
  5.0 0.9 copy.16.wd
  5.9 190.3 %shard_map.118 = (bf16[128,256]{1,0:T(8,128)(2,1)}, bf16[128,256]{1,0:T(8,128)(2,1)}, f32[1,128]{1,0:T(1,128)}, f32[256,704]{1,0:T(8,128)}, f32[256,704]{1,0:T(8,128)}, /*index=5*/f32[256,704]{1,0:T(8,128)}) custom-call(bf16[128,1024]{1,0:T(8,128)(2,1)} %tok.1, bf16[128,1024]{1,0:T(8,128)(2,1)} %cot.1, s32[128,1]{1,0:T(8,128)} %copy.13.ids, ...), custom_call_target="tpu_custom_call" | custom-call | tf_op jit(solution)/shard_map/pallas_call | solution.py:376
  196.2 0.0 copy-start.1
  196.2 2.3 %copy.17 = f32[256,704]{0,1:T(8,128)} copy(f32[256,704]{1,0:T(8,128)} %get-tuple-element.21) | data formatting | bytes 1441792
  198.5 0.0 copy-done.1
  198.5 0.0 copy-start
  198.5 1.1 copy.18
  199.6 0.0 copy-done
  199.7 0.0 copy-start.5
  199.7 1.1 copy.19
  200.8 0.0 copy-done.5
  200.8 0.0 copy-start.4
  200.8 0.6 copy.23
  201.4 0.2 copy-done.4
  201.6 0.0 copy-start.7
  201.6 0.6 copy.24
  202.3 0.0 copy-done.7
  202.3 0.5 copy.25
Async XLA Ops:
  0.6 0.7 copy-start.6
  2.0 2.0 copy-start.2
  4.0 1.0 copy-start.3
  196.2 2.3 %copy-start.1 = (f32[256,704]{1,0:T(8,128)S(1)}, f32[256,704]{1,0:T(8,128)}, u32[]{:S(2)}) copy-start(f32[256,704]{1,0:T(8,128)} %get-tuple-element.22) | copy-start | bytes 2162692
  198.5 1.1 copy-start
  199.7 1.1 copy-start.5
  200.8 0.9 copy-start.4
  201.6 0.7 copy-start.7

commit v2 on v1

v2 whole, which is shorter than its diff:
```python
import functools

import jax
import jax.numpy as jnp
from jax import lax
from jax.experimental import pallas as pl
from jax.experimental.pallas import tpu as pltpu
from jax.sharding import PartitionSpec as P

CAP = 16
F32 = jnp.float32
BF16 = jnp.bfloat16


def dot(a, b):
    return lax.dot_general(a, b, (((1,), (0,)), ((), ())), preferred_element_type=F32)


def dot_t(a, b):
    return lax.dot_general(a, b, (((1,), (1,)), ((), ())), preferred_element_type=F32)


def cuts(ff):
    step = ff // 4 if ff % 64 == 0 else ff
    return [(low, step) for low in range(0, ff, step)]


def piece_count(blocks):
    return min(4, blocks)


def kernel(
    tok, cot, ids, prob, wg, wu, wd,
    o_out, o_grad, o_prob, o_gg, o_gu, o_gd,
    wall, sendbuf, x4, act_t, pre, act3, out_acc, in_acc, gloc, r_right, r_left, stage,
    t1s, t1r, t2s, t2r, fo, back, place, probs, parts,
    ag_send, ag_recv, rs_send, rs_recv, a_send, a_recv, l_sem, n_send, n_recv,
    t1_send, t1_recv, t2_send, t2_recv, b_send, b_recv, p_send, p_recv, o_sem, enter,
):
    toks, width = tok.shape
    _, _, ff, quarter = wall.shape
    chunks = cuts(ff)
    nf = len(chunks)
    experts = sendbuf.shape[0] // CAP
    rows = x4.shape[1]
    blocks = rows // CAP
    pieces = piece_count(blocks)
    piece_blocks = blocks // pieces
    piece_rows = rows // pieces
    turns = (0, 1, 3, 2)[:pieces] if pieces > 2 else tuple(range(pieces))
    x_size = min(4, experts // 2)
    y_size = experts // 2 // x_size
    me = lax.axis_index("wide")
    n = lax.axis_index("narrow")
    m = lax.rem(me, 4)
    e0 = lax.div(me, 4)
    half = lax.rem(e0, 2)
    group = lax.div(me, 8)
    i0 = group * 2
    own_piece = lax.div(i0, piece_blocks)
    x_at, y_at, z_at = lax.rem(group, x_size), lax.div(group, x_size), lax.rem(me, 8)
    core_peer = n + 1 - 2 * lax.rem(n, 2)
    row_peer = lax.rem(n + 2, 4)
    far_peer = 3 - n

    def dest_of(e):
        h = lax.rem(e + half, 2)
        return 4 * e + m + h * (3 - 2 * m), i0 + h

    def source_of(i):
        h = lax.rem(i, 2)
        return lax.div(i, 2) * 8 + lax.rem(half + h, 2) * 4 + m + h * (3 - 2 * m)

    def remote(src, dst, ssem, rsem, wide, narrow):
        return pltpu.make_async_remote_copy(
            src_ref=src, dst_ref=dst, send_sem=ssem, recv_sem=rsem,
            device_id={"wide": wide, "narrow": narrow}, device_id_type=pl.DeviceIdType.MESH,
        )

    def await_bytes(ref, sem):
        pltpu.make_async_copy(ref, ref, sem).wait()

    owned = [
        pltpu.make_async_copy(ref, wall.at[m, k], l_sem.at[2 + k])
        for k, ref in enumerate((wg, wu, wd))
    ]
    for copy in owned:
        copy.start()

    barrier = pltpu.get_barrier_semaphore()

    def signal(wide, narrow):
        pl.semaphore_signal(
            barrier, inc=1, device_id={"wide": wide, "narrow": narrow},
            device_id_type=pl.DeviceIdType.MESH,
        )

    for turn in range(1, 8):
        signal(8 * group + lax.rem(z_at + turn, 8), n)
    for peer in (core_peer, row_peer, far_peer):
        signal(me, peer)
    along_x = [
        (y_at * x_size + lax.rem(x_at + turn, x_size)) * 8 + z_at for turn in range(1, x_size)
    ]
    along_y = [
        (lax.rem(y_at + turn, y_size) * x_size + x_at) * 8 + z_at for turn in range(1, y_size)
    ]
    for peer in (*along_x, *along_y):
        signal(peer, n)

    def piece(ref, f, q):
        low, size = chunks[f]
        return ref.at[q, :, pl.ds(low, size)]

    def ag_right(f, q):
        return remote(
            piece(wall, f, q), piece(wall, f, q), ag_send.at[0, f, q], ag_recv.at[f, q], me + 1, n
        )

    def ag_left(f, q):
        return remote(
            piece(wall, f, q), piece(wall, f, q), ag_send.at[1, f, q], ag_recv.at[f, q], me - 1, n
        )

    def ag_own(f):
        @pl.when(m < 3)
        def _():
            ag_right(f, m).start()

        @pl.when(m > 0)
        def _():
            ag_left(f, m).start()

    def ag_await(f, q):
        await_bytes(piece(wall, f, q), ag_recv.at[f, q])

    def ag_late(fs):
        for f in fs:
            @pl.when(m == 0)
            def _():
                ag_right(f, 0).start()

            @pl.when(m == 3)
            def _():
                ag_left(f, 3).start()

    def mid_fill(f):
        for own, near, send, back_near, back_far, send_back in (
            (1, 0, ag_right, 2, 3, ag_left),
            (2, 3, ag_left, 1, 0, ag_right),
        ):
            @pl.when(m == own)
            def _():
                ag_await(f, near)
                send(f, near).start()
                if f + 2 < nf:
                    send(f + 2, own).start()
                ag_await(f, back_near)
                send_back(f, back_near).start()
                ag_await(f, back_far)
                send_back(f, back_far).start()
                if f + 2 < nf:
                    send_back(f + 2, own).start()

    def end_fill(f):
        for own, others in ((0, (1, 2, 3)), (3, (2, 1, 0))):
            @pl.when(m == own)
            def _():
                for q in others:
                    ag_await(f, q)

    def pass_on(sem, peers):
        for peer in peers:
            pl.semaphore_signal(
                sem, inc=1, device_id={"wide": peer, "narrow": n},
                device_id_type=pl.DeviceIdType.MESH,
            )

    for copy in owned:
        copy.wait()
    pl.semaphore_wait(barrier, 10 + len(along_x) + len(along_y))
    pass_on(enter.at[0], along_x)
    ag_own(0)
    ag_own(1)

    def iota(shape, axis):
        return lax.broadcasted_iota(jnp.int32, shape, axis).astype(F32)

    slots = experts * CAP
    row_i, col_i = iota((toks, toks), 0), iota((toks, toks), 1)
    diag = row_i == col_i
    idf = ids[...].astype(F32)
    onehot = jnp.where(iota((experts, toks), 0) == idf, 1.0, 0.0)
    before = jnp.where(row_i < col_i, 1.0, 0.0).astype(BF16)
    rank = jnp.sum(dot(onehot.astype(BF16), before) * onehot, axis=0, keepdims=True)
    slot_row = idf * CAP + rank
    slot = jnp.sum(jnp.where(diag, slot_row, 0.0), axis=1, keepdims=True)
    place[...] = jnp.where(iota((toks, slots), 1) == slot, 1.0, 0.0).astype(BF16)
    prob_col = jnp.sum(jnp.where(diag, prob[...], 0.0), axis=1, keepdims=True)
    probs[...] = jnp.broadcast_to(prob_col, (toks, quarter))
    columns = pl.ds(pl.multiple_of(n * quarter, quarter), quarter)
    pick = jnp.where(iota((slots, toks), 0) == slot_row, 1.0, 0.0).astype(BF16)
    scaled = (prob_col * cot[:, columns].astype(F32)).astype(BF16)
    sendbuf[:, :quarter] = dot(pick, tok[:, columns]).astype(BF16)
    sendbuf[:, quarter:] = dot(pick, scaled).astype(BF16)

    if along_x:
        pl.semaphore_wait(enter.at[0], len(along_x))
    if along_y:
        pass_on(enter.at[1], along_y)
        pl.semaphore_wait(enter.at[1], len(along_y))

    def rows_at(i):
        return pl.ds(pl.multiple_of(i * CAP, CAP), CAP)

    def rows_of(p):
        return pl.ds(pl.multiple_of(p * piece_rows, piece_rows), piece_rows)

    def piece_at(turn):
        return lax.rem(own_piece + turn, pieces)

    pltpu.make_async_copy(
        sendbuf.at[rows_at(e0)], x4.at[n, rows_at(i0)], a_recv.at[own_piece]
    ).start()

    @pl.loop(1, experts)
    def _(j):
        e = lax.rem(e0 + j, experts)
        wide, block = dest_of(e)
        remote(
            sendbuf.at[rows_at(e)], x4.at[n, rows_at(block)], a_send, a_recv.at[own_piece], wide, n
        ).start()

    def x_copy(k, slot, turn, peer):
        part = x4.at[slot, rows_of(piece_at(turn))]
        return remote(
            part, part, n_send.at[k, piece_at(turn)], n_recv.at[slot, piece_at(turn)], me, peer
        )

    def x_await(slot, turn):
        p = piece_at(turn)
        await_bytes(x4.at[slot, rows_of(p)], n_recv.at[slot, p])

    x_sent = []

    def x_share(turn):
        await_bytes(x4.at[n, rows_of(piece_at(turn))], a_recv.at[piece_at(turn)])
        for k, peer in ((1, row_peer), (0, core_peer)):
            copy = x_copy(k, n, turn, peer)
            copy.start()
            x_sent.append(copy)

    def x_relay(turn):
        x_await(row_peer, turn)
        copy = x_copy(2, row_peer, turn, core_peer)
        copy.start()
        x_sent.append(copy)

    out_acc[...] = jnp.zeros_like(out_acc)
    in_acc[...] = jnp.zeros_like(in_acc)
    ag_late(range(2, nf))
    mid_fill(0)
    for turn in turns:
        x_share(turn)
    mid_fill(1)
    for turn in turns:
        x_relay(turn)
    for slot in (core_peer, far_peer):
        for turn in turns:
            x_await(slot, turn)

    def rs_right(f, q):
        return remote(
            piece(stage, f, q), piece(r_right, f, q), rs_send.at[f, q], rs_recv.at[0, f, q], me + 1, n
        )

    def rs_left(f, q):
        return remote(
            piece(stage, f, q), piece(r_left, f, q), rs_send.at[f, q], rs_recv.at[1, f, q], me - 1, n
        )

    def rs_first(f):
        low, size = chunks[f]
        part = pl.ds(low, size)

        @pl.when(m == 0)
        def _():
            for q in (3, 2, 1):
                stage[q, :, part] = gloc[q, :, part].astype(BF16)
                rs_right(f, q).start()

        @pl.when(m == 3)
        def _():
            for q in (0, 1, 2):
                stage[q, :, part] = gloc[q, :, part].astype(BF16)
                rs_left(f, q).start()

    def relay(f, source, k, q, send):
        low, size = chunks[f]
        part = pl.ds(low, size)
        await_bytes(piece(source, f, q), rs_recv.at[k, f, q])
        stage[q, :, part] = (gloc[q, :, part] + source[q, :, part].astype(F32)).astype(BF16)
        send(f, q).start()

    def relay_a(f, k):
        @pl.when(m == 1)
        def _():
            relay(f, r_right, 0, 3 - k, rs_right)

        @pl.when(m == 2)
        def _():
            relay(f, r_left, 1, k, rs_left)

    def relay_b(f):
        @pl.when(m == 1)
        def _():
            relay(f, r_left, 1, 0, rs_left)

        @pl.when(m == 2)
        def _():
            relay(f, r_right, 0, 3, rs_right)

    step_rows = min(64, rows)
    eye = jnp.where(iota((256, 256), 0) == iota((256, 256), 1), 1.0, 0.0).astype(BF16)

    for f, (low, size) in enumerate(chunks):
        end_fill(f)
        units = pl.ds(low, size)
        for k, first in ((0, 0), (1, 0), (2, quarter)):
            total = dot_t(x4[0, :, first : first + quarter], wall[0, k, units])
            for q in range(1, 4):
                total += dot_t(x4[q, :, first : first + quarter], wall[q, k, units])
            pre[k, :, :size] = total

        @pl.loop(0, rows // step_rows)
        def _(r):
            part = pl.ds(pl.multiple_of(r * step_rows, step_rows), step_rows)
            gate, up, d_hidden = pre[0, part, :size], pre[1, part, :size], pre[2, part, :size]
            sigma = jax.nn.sigmoid(gate)
            active = gate * sigma
            d_gate = d_hidden * up * sigma * (1.0 + gate * (1.0 - sigma))
            act3[0, part, :size] = (active * up).astype(BF16)
            act3[1, part, :size] = d_gate.astype(BF16)
            act3[2, part, :size] = (d_hidden * active).astype(BF16)

        for k in range(3):
            act_t[k, :size] = dot_t(eye[:size, :size], act3[k, :, :size]).astype(BF16)

        @pl.loop(0, 4)
        def _(q):
            gloc[q, 0, units] = dot(act_t[1, :size], x4[q, :, :quarter])
            gloc[q, 1, units] = dot(act_t[2, :size], x4[q, :, :quarter])
            gloc[q, 2, units] = dot(act_t[0, :size], x4[q, :, quarter:])

        rs_first(f)

        @pl.loop(0, 4)
        def _(q):
            out_acc[q] += dot(act3[0, :, :size], wall[q, 2, units])
            in_acc[q] += dot(act3[1, :, :size], wall[q, 0, units]) + dot(
                act3[2, :, :size], wall[q, 1, units]
            )

        if f + 2 < nf:
            mid_fill(f + 2)
        if f == nf - 2:
            for k in range(2):
                relay_a(0, k)

    def both(q, part):
        return jnp.concatenate([out_acc[q, part], in_acc[q, part]], axis=1)

    back_turns = (2, 1, 3, 0) if pieces == 4 else turns
    t1, t2 = {}, {}
    for k, q in ((1, far_peer), (0, core_peer)):
        for turn in back_turns:
            p = piece_at(turn)
            part = rows_of(p)
            t1s[k, part] = both(q, part).astype(BF16)
            t1[k, turn] = remote(
                t1s.at[k, part], t1r.at[k, part], t1_send.at[k, p], t1_recv.at[k, p], me, core_peer
            )
            t1[k, turn].start()
    for k in range(2):
        relay_a(1, k)
    for turn in back_turns:
        p = piece_at(turn)
        part = rows_of(p)
        t1[1, turn].wait_recv()
        t2s[part] = (both(row_peer, part) + t1r[1, part].astype(F32)).astype(BF16)
        t2[turn] = remote(t2s.at[part], t2r.at[part], t2_send.at[p], t2_recv.at[p], me, row_peer)
        t2[turn].start()

    def send_back(turn):
        p = piece_at(turn)
        part = rows_of(p)
        t1[0, turn].wait_recv()
        t2[turn].wait_recv()
        total = both(n, part) + t1r[0, part].astype(F32) + t2r[part].astype(F32)
        fo[part] = total.astype(BF16)

        @pl.loop(0, piece_blocks)
        def _(j):
            i = p * piece_blocks + j

            @pl.when(i == i0)
            def _():
                pltpu.make_async_copy(fo.at[rows_at(i)], back.at[rows_at(e0)], b_recv).start()

            @pl.when(i != i0)
            def _():
                remote(
                    fo.at[rows_at(i)], back.at[rows_at(e0)], b_send, b_recv, source_of(i), n
                ).start()

    half_turns = len(back_turns) // 2
    relay_b(0)
    for turn in back_turns[:half_turns]:
        send_back(turn)
    relay_b(1)
    for turn in back_turns[half_turns:]:
        send_back(turn)
    for f in range(2, nf):
        for k in range(2):
            relay_a(f, k)
        if f < nf - 1:
            relay_b(f)
    relay_b(nf - 1)

    written = []

    def finish(f):
        low, size = chunks[f]
        part = pl.ds(low, size)

        @pl.when(m > 0)
        def _():
            await_bytes(piece(r_right, f, m), rs_recv.at[0, f, m])
            gloc[m, :, part] += r_right[m, :, part].astype(F32)

        @pl.when(m < 3)
        def _():
            await_bytes(piece(r_left, f, m), rs_recv.at[1, f, m])
            gloc[m, :, part] += r_left[m, :, part].astype(F32)

        for k, ref in enumerate((o_gg, o_gu, o_gd)):
            copy = pltpu.make_async_copy(gloc.at[m, k, part], ref.at[part], o_sem.at[k, f])
            copy.start()
            written.append(copy)

    for f in range(nf - 1):
        finish(f)

    await_bytes(back, b_recv)
    ffn = dot(place[...], back[:, :quarter])
    o_out[...] = (probs[...] * ffn).astype(BF16)
    o_grad[...] = dot(place[...], back[:, quarter:]).astype(BF16)
    part_col = jnp.sum(ffn * cot[:, columns].astype(F32), axis=1, keepdims=True)
    part_row = jnp.sum(jnp.where(diag, part_col, 0.0), axis=0, keepdims=True)
    parts[n] = jnp.broadcast_to(part_row, parts.shape[1:])
    sent = []
    for k, peer in enumerate((core_peer, row_peer, far_peer)):
        copy = remote(parts.at[n], parts.at[n], p_send.at[k], p_recv.at[n], me, peer)
        copy.start()
        sent.append(copy)
    finish(nf - 1)
    for peer in (core_peer, row_peer, far_peer):
        await_bytes(parts.at[peer], p_recv.at[peer])
    o_prob[...] = (parts[0] + parts[1] + parts[2] + parts[3])[:1]

    for copy in (*sent, *x_sent, *t1.values(), *t2.values()):
        copy.wait_send()
    for copy in written:
        copy.wait()
    await_bytes(sendbuf.at[pl.ds(0, slots - CAP)], a_send)
    await_bytes(fo.at[pl.ds(0, rows - CAP)], b_send)

    for f in range(nf):
        for q in range(4):
            @pl.when(m != q)
            def _():
                await_bytes(piece(stage, f, q), rs_send.at[f, q])

            @pl.when((m < 3) & (m >= q))
            def _():
                await_bytes(piece(wall, f, q), ag_send.at[0, f, q])

            @pl.when((m > 0) & (m <= q))
            def _():
                await_bytes(piece(wall, f, q), ag_send.at[1, f, q])


def shards(wide, tokens, cotangent, expert_ids, route_prob, gate_weight, up_weight, down_weight):
    toks, width = tokens.shape
    quarter, ff = gate_weight.shape
    experts = wide // 4
    slots = experts * CAP
    rows = wide // 4 * CAP
    nf = len(cuts(ff))
    chunk = cuts(ff)[0][1]
    pieces = piece_count(experts)
    any_spec = pl.BlockSpec(memory_space=pl.ANY)
    vmem, dma = pltpu.VMEM, pltpu.SemaphoreType.DMA
    spec = pl.BlockSpec(memory_space=pltpu.VMEM)
    grad = jax.ShapeDtypeStruct((ff, quarter), F32)
    two = 2 * quarter
    outs = pl.pallas_call(
        kernel,
        out_shape=(
            jax.ShapeDtypeStruct((toks, quarter), BF16),
            jax.ShapeDtypeStruct((toks, quarter), BF16),
            jax.ShapeDtypeStruct((1, toks), F32),
            grad, grad, grad,
        ),
        in_specs=[spec] * 4 + [any_spec] * 3,
        out_specs=(spec,) * 3 + (any_spec,) * 3,
        scratch_shapes=[
            vmem((4, 3, ff, quarter), BF16),
            vmem((slots, two), BF16),
            vmem((4, rows, two), BF16),
            vmem((3, chunk, rows), BF16),
            vmem((3, rows, chunk), F32),
            vmem((3, rows, chunk), BF16),
            vmem((4, rows, quarter), F32),
            vmem((4, rows, quarter), F32),
            vmem((4, 3, ff, quarter), F32),
            vmem((4, 3, ff, quarter), BF16),
            vmem((4, 3, ff, quarter), BF16),
            vmem((4, 3, ff, quarter), BF16),
            vmem((2, rows, two), BF16),
            vmem((2, rows, two), BF16),
            vmem((rows, two), BF16),
            vmem((rows, two), BF16),
            vmem((rows, two), BF16),
            vmem((slots, two), BF16),
            vmem((toks, slots), BF16),
            vmem((toks, quarter), F32),
            vmem((4, 8, toks), F32),
            dma((2, nf, 4)), dma((nf, 4)), dma((nf, 4)), dma((2, nf, 4)),
            dma, dma((pieces,)), dma((5,)), dma((3, pieces)), dma((4, pieces)),
            dma((2, pieces)), dma((2, pieces)), dma((pieces,)), dma((pieces,)),
            dma, dma, dma((3,)), dma((4,)), dma((3, nf)), pltpu.SemaphoreType.REGULAR((2,)),
        ],
        compiler_params=pltpu.CompilerParams(
            collective_id=0, has_side_effects=True, vmem_limit_bytes=63000 * 1024
        ),
    )(
        tokens, cotangent, expert_ids.reshape(1, toks), route_prob.reshape(1, toks),
        gate_weight.T, up_weight.T, down_weight.T,
    )
    return outs[0], outs[1], outs[2].reshape(toks), outs[3].T, outs[4].T, outs[5].T


def solution(mesh):
    in_specs = (
        P("wide", None),
        P("wide", None),
        P("wide", None),
        P("wide"),
        P("wide", "narrow"),
        P("wide", "narrow"),
        P("wide", "narrow"),
    )
    out_specs = (
        P("wide", "narrow"),
        P("wide", "narrow"),
        P("wide"),
        P("wide", "narrow"),
        P("wide", "narrow"),
        P("wide", "narrow"),
    )
    return jax.shard_map(
        functools.partial(shards, mesh.shape["wide"]),
        mesh=mesh, in_specs=in_specs, out_specs=out_specs, check_vma=False,
    )
```

time: 206 us -> 141 us (0.68); the launches traced: 203 us -> 141 us
  Pallas kernels: 190 us -> 133 us
  local copies, waits for them, and re-layouts: 11.9 us -> 6.97 us
    pallas_call x1, Pallas kernels: 190 us -> 133 us  [shards(): pl.pallas_call(kernel, out_shape=(jax.ShapeDtypeStruct((toks, quarter), B...]
    unnamed x26 -> x14, local copies, waits for them, and re-layouts: 11.9 us -> 6.97 us
where the time goes in v2:
time: 141 us
  Pallas kernels  133 us (94%)
  local copies, waits for them, and re-layouts  6.97 us (5%)
    pallas_call x1, Pallas kernels, shards(): pl.pallas_call(kernel, out_shape=(jax.ShapeDtypeStruct((toks, quarter), B...  133 us
    unnamed x14, local copies, waits for them, and re-layouts  6.97 us

profile of v2, /device:TPU:1, one launch (start us, length us, event | category | flops | bytes accessed | tf_op | source)
XLA Modules:
  0.0 140.8 jit_solution(11059902633059139533)
XLA Ops:
  0.6 133.2 %shard_map.118 = (bf16[128,256]{1,0:T(8,128)(2,1)}, bf16[128,256]{1,0:T(8,128)(2,1)}, f32[1,128]{1,0:T(1,128)}, f32[704,256]{1,0:T(8,128)}, f32[704,256]{1,0:T(8,128)}, /*index=5*/f32[704,256]{1,0:T(8,128)}) custom-call(bf16[128,1024]{1,0:T(8,128)(2,1)} %tok.1, bf16[128,1024]{1,0:T(8,128)(2,1)} %cot.1, s32[1,128]{1,0:T(1,128)} %bitcast.15, ...), custom_call_target="tpu_custom_call" | custom-call | tf_op jit(solution)/shard_map/pallas_call | solution.py:507
  133.8 0.0 copy-start.2
  133.9 1.5 %copy.19 = bf16[128,256]{1,0:T(8,128)(2,1)} copy(bf16[128,256]{1,0:T(8,128)(2,1)} %get-tuple-element.24) | data formatting | bytes 131072
  135.4 0.0 copy-done.2
  135.4 0.0 copy-start.3
  135.4 0.6 copy.20
  136.0 0.0 copy-done.3
  136.0 0.5 copy.21
  136.5 0.0 copy-start.1
  136.5 2.1 %copy.22 = f32[256,704]{0,1:T(8,128)} copy(f32[256,704]{0,1:T(8,128)} %bitcast.11) | data formatting | bytes 1441792
  138.6 0.0 copy-done.1
  138.6 0.0 copy-start
  138.6 0.9 copy.23
  139.5 0.5 copy-done
  140.0 0.9 copy.24
Async XLA Ops:
  133.8 1.5 %copy-start.2 = (bf16[128,256]{1,0:T(8,128)(2,1)S(1)}, bf16[128,256]{1,0:T(8,128)(2,1)}, u32[]{:S(2)}) copy-start(bf16[128,256]{1,0:T(8,128)(2,1)} %get-tuple-element.25) | copy-start | bytes 196612
  135.4 0.6 copy-start.3
  136.5 2.1 %copy-start.1 = (f32[704,256]{1,0:T(8,128)S(1)}, f32[704,256]{1,0:T(8,128)}, u32[]{:S(2)}) copy-start(f32[704,256]{1,0:T(8,128)} %get-tuple-element.16) | copy-start | bytes 2162692
  138.6 1.4 copy-start

commit v3 on v2

--- a/solution.py
+++ b/solution.py
@@ -21,7 +21,7 @@
 
 
 def cuts(ff):
-    step = ff // 4 if ff % 64 == 0 else ff
+    step = ff // 4
     return [(low, step) for low in range(0, ff, step)]
 
 
@@ -31,9 +31,9 @@
 
 def kernel(
     tok, cot, ids, prob, wg, wu, wd,
-    o_out, o_grad, o_prob, o_gg, o_gu, o_gd,
+    o_rows, o_prob, o_weights,
     wall, sendbuf, x4, act_t, pre, act3, out_acc, in_acc, gloc, r_right, r_left, stage,
-    t1s, t1r, t2s, t2r, fo, back, place, probs, parts,
+    t1s, t1r, t2s, t2r, fo, back, place, probs, parts, rows_out, prob_out,
     ag_send, ag_recv, rs_send, rs_recv, a_send, a_recv, l_sem, n_send, n_recv,
     t1_send, t1_recv, t2_send, t2_recv, b_send, b_recv, p_send, p_recv, o_sem, enter,
 ):
@@ -144,23 +144,29 @@
             def _():
                 ag_left(f, 3).start()
 
-    def mid_fill(f):
-        for own, near, send, back_near, back_far, send_back in (
-            (1, 0, ag_right, 2, 3, ag_left),
-            (2, 3, ag_left, 1, 0, ag_right),
-        ):
+    middle = (
+        (1, 0, ag_right, 2, 3, ag_left),
+        (2, 3, ag_left, 1, 0, ag_right),
+    )
+
+    def near_fill(f):
+        for own, near, send, _, _, _ in middle:
             @pl.when(m == own)
             def _():
                 ag_await(f, near)
                 send(f, near).start()
                 if f + 2 < nf:
                     send(f + 2, own).start()
-                ag_await(f, back_near)
-                send_back(f, back_near).start()
-                ag_await(f, back_far)
-                send_back(f, back_far).start()
+
+    def back_fill(f):
+        for own, _, _, near, far, send in middle:
+            @pl.when(m == own)
+            def _():
+                for q in (near, far):
+                    ag_await(f, q)
+                    send(f, q).start()
                 if f + 2 < nf:
-                    send_back(f + 2, own).start()
+                    send(f + 2, own).start()
 
     def end_fill(f):
         for own, others in ((0, (1, 2, 3)), (3, (2, 1, 0))):
@@ -176,12 +182,15 @@
                 device_id_type=pl.DeviceIdType.MESH,
             )
 
+    pl.semaphore_wait(barrier, 10 + len(along_x) + len(along_y))
+    pass_on(enter.at[0], along_x)
     for copy in owned:
         copy.wait()
-    pl.semaphore_wait(barrier, 10 + len(along_x) + len(along_y))
-    pass_on(enter.at[0], along_x)
     ag_own(0)
     ag_own(1)
+    if along_x:
+        pl.semaphore_wait(enter.at[0], len(along_x))
+    pass_on(enter.at[1], along_y)
 
     def iota(shape, axis):
         return lax.broadcasted_iota(jnp.int32, shape, axis).astype(F32)
@@ -204,10 +213,7 @@
     sendbuf[:, :quarter] = dot(pick, tok[:, columns]).astype(BF16)
     sendbuf[:, quarter:] = dot(pick, scaled).astype(BF16)
 
-    if along_x:
-        pl.semaphore_wait(enter.at[0], len(along_x))
     if along_y:
-        pass_on(enter.at[1], along_y)
         pl.semaphore_wait(enter.at[1], len(along_y))
 
     def rows_at(i):
@@ -223,13 +229,15 @@
         sendbuf.at[rows_at(e0)], x4.at[n, rows_at(i0)], a_recv.at[own_piece]
     ).start()
 
-    @pl.loop(1, experts)
-    def _(j):
+    def send_block(j):
         e = lax.rem(e0 + j, experts)
         wide, block = dest_of(e)
         remote(
             sendbuf.at[rows_at(e)], x4.at[n, rows_at(block)], a_send, a_recv.at[own_piece], wide, n
         ).start()
+
+    pl.loop(experts // 2, experts)(send_block)
+    pl.loop(1, experts // 2)(send_block)
 
     def x_copy(k, slot, turn, peer):
         part = x4.at[slot, rows_of(piece_at(turn))]
@@ -258,13 +266,17 @@
 
     out_acc[...] = jnp.zeros_like(out_acc)
     in_acc[...] = jnp.zeros_like(in_acc)
-    ag_late(range(2, nf))
-    mid_fill(0)
+    near_fill(0)
+    back_fill(0)
     for turn in turns:
         x_share(turn)
-    mid_fill(1)
+    ag_late(range(2, nf))
+    near_fill(1)
+    back_fill(1)
     for turn in turns:
         x_relay(turn)
+    near_fill(2)
+    near_fill(3)
     for slot in (core_peer, far_peer):
         for turn in turns:
             x_await(slot, turn)
@@ -279,21 +291,14 @@
             piece(stage, f, q), piece(r_left, f, q), rs_send.at[f, q], rs_recv.at[1, f, q], me - 1, n
         )
 
-    def rs_first(f):
+    def rs_first(f, q):
         low, size = chunks[f]
         part = pl.ds(low, size)
-
-        @pl.when(m == 0)
-        def _():
-            for q in (3, 2, 1):
+        for own, send in ((0, rs_right), (3, rs_left)):
+            @pl.when((m == own) & (q != own))
+            def _():
                 stage[q, :, part] = gloc[q, :, part].astype(BF16)
-                rs_right(f, q).start()
-
-        @pl.when(m == 3)
-        def _():
-            for q in (0, 1, 2):
-                stage[q, :, part] = gloc[q, :, part].astype(BF16)
-                rs_left(f, q).start()
+                send(f, q).start()
 
     def relay(f, source, k, q, send):
         low, size = chunks[f]
@@ -319,6 +324,22 @@
         @pl.when(m == 2)
         def _():
             relay(f, r_right, 0, 3, rs_right)
+
+    def both(q, part):
+        return jnp.concatenate([out_acc[q, part], in_acc[q, part]], axis=1)
+
+    back_turns = (2, 1, 3, 0) if pieces == 4 else turns
+    t1, t2 = {}, {}
+
+    def share_on_chip(k, q):
+        for turn in back_turns:
+            p = piece_at(turn)
+            part = rows_of(p)
+            t1s[k, part] = both(q, part).astype(BF16)
+            t1[k, turn] = remote(
+                t1s.at[k, part], t1r.at[k, part], t1_send.at[k, p], t1_recv.at[k, p], me, core_peer
+            )
+            t1[k, turn].start()
 
     step_rows = min(64, rows)
     eye = jnp.where(iota((256, 256), 0) == iota((256, 256), 1), 1.0, 0.0).astype(BF16)
@@ -343,46 +364,44 @@
             act3[1, part, :size] = d_gate.astype(BF16)
             act3[2, part, :size] = (d_hidden * active).astype(BF16)
 
-        for k in range(3):
-            act_t[k, :size] = dot_t(eye[:size, :size], act3[k, :, :size]).astype(BF16)
-
-        @pl.loop(0, 4)
-        def _(q):
-            gloc[q, 0, units] = dot(act_t[1, :size], x4[q, :, :quarter])
-            gloc[q, 1, units] = dot(act_t[2, :size], x4[q, :, :quarter])
-            gloc[q, 2, units] = dot(act_t[0, :size], x4[q, :, quarter:])
-
-        rs_first(f)
-
-        @pl.loop(0, 4)
-        def _(q):
+        def transpose():
+            for k in range(3):
+                act_t[k, :size] = dot_t(eye[:size, :size], act3[k, :, :size]).astype(BF16)
+
+        def gradients():
+            @pl.loop(0, 4)
+            def _(step):
+                q = step + lax.div(3 - m, 2) * (3 - 2 * step)
+                gloc[q, 0, units] = dot(act_t[1, :size], x4[q, :, :quarter])
+                gloc[q, 1, units] = dot(act_t[2, :size], x4[q, :, :quarter])
+                gloc[q, 2, units] = dot(act_t[0, :size], x4[q, :, quarter:])
+                rs_first(f, q)
+
+        def row_sum(q):
             out_acc[q] += dot(act3[0, :, :size], wall[q, 2, units])
             in_acc[q] += dot(act3[1, :, :size], wall[q, 0, units]) + dot(
                 act3[2, :, :size], wall[q, 1, units]
             )
 
-        if f + 2 < nf:
-            mid_fill(f + 2)
-        if f == nf - 2:
-            for k in range(2):
-                relay_a(0, k)
-
-    def both(q, part):
-        return jnp.concatenate([out_acc[q, part], in_acc[q, part]], axis=1)
-
-    back_turns = (2, 1, 3, 0) if pieces == 4 else turns
-    t1, t2 = {}, {}
-    for k, q in ((1, far_peer), (0, core_peer)):
-        for turn in back_turns:
-            p = piece_at(turn)
-            part = rows_of(p)
-            t1s[k, part] = both(q, part).astype(BF16)
-            t1[k, turn] = remote(
-                t1s.at[k, part], t1r.at[k, part], t1_send.at[k, p], t1_recv.at[k, p], me, core_peer
-            )
-            t1[k, turn].start()
-    for k in range(2):
-        relay_a(1, k)
+        if f < nf - 1:
+            transpose()
+            gradients()
+            pl.loop(0, 4)(row_sum)
+        else:
+            for k, q in ((1, far_peer), (0, core_peer)):
+                row_sum(q)
+                share_on_chip(k, q)
+            row_sum(row_peer)
+            row_sum(n)
+            transpose()
+            gradients()
+        if f < 2:
+            relay_a(f, 0)
+            back_fill(f + 2)
+            relay_a(f, 1)
+        if f == 2:
+            relay_b(0)
+
     for turn in back_turns:
         p = piece_at(turn)
         part = rows_of(p)
@@ -413,18 +432,15 @@
                     fo.at[rows_at(i)], back.at[rows_at(e0)], b_send, b_recv, source_of(i), n
                 ).start()
 
-    half_turns = len(back_turns) // 2
-    relay_b(0)
-    for turn in back_turns[:half_turns]:
+    relay_a(2, 0)
+    relay_b(1)
+    relay_a(2, 1)
+    for turn in back_turns:
+        if turn == back_turns[-1]:
+            relay_b(2)
+            relay_a(3, 0)
         send_back(turn)
-    relay_b(1)
-    for turn in back_turns[half_turns:]:
-        send_back(turn)
-    for f in range(2, nf):
-        for k in range(2):
-            relay_a(f, k)
-        if f < nf - 1:
-            relay_b(f)
+    relay_a(3, 1)
     relay_b(nf - 1)
 
     written = []
@@ -443,18 +459,20 @@
             await_bytes(piece(r_left, f, m), rs_recv.at[1, f, m])
             gloc[m, :, part] += r_left[m, :, part].astype(F32)
 
-        for k, ref in enumerate((o_gg, o_gu, o_gd)):
-            copy = pltpu.make_async_copy(gloc.at[m, k, part], ref.at[part], o_sem.at[k, f])
-            copy.start()
-            written.append(copy)
+        copy = pltpu.make_async_copy(gloc.at[m, :, part], o_weights.at[:, part], o_sem.at[f])
+        copy.start()
+        written.append(copy)
 
     for f in range(nf - 1):
         finish(f)
 
     await_bytes(back, b_recv)
     ffn = dot(place[...], back[:, :quarter])
-    o_out[...] = (probs[...] * ffn).astype(BF16)
-    o_grad[...] = dot(place[...], back[:, quarter:]).astype(BF16)
+    rows_out[0] = (probs[...] * ffn).astype(BF16)
+    rows_out[1] = dot(place[...], back[:, quarter:]).astype(BF16)
+    copy = pltpu.make_async_copy(rows_out, o_rows, l_sem.at[0])
+    copy.start()
+    written.append(copy)
     part_col = jnp.sum(ffn * cot[:, columns].astype(F32), axis=1, keepdims=True)
     part_row = jnp.sum(jnp.where(diag, part_col, 0.0), axis=0, keepdims=True)
     parts[n] = jnp.broadcast_to(part_row, parts.shape[1:])
@@ -463,10 +481,13 @@
         copy = remote(parts.at[n], parts.at[n], p_send.at[k], p_recv.at[n], me, peer)
         copy.start()
         sent.append(copy)
-    finish(nf - 1)
     for peer in (core_peer, row_peer, far_peer):
         await_bytes(parts.at[peer], p_recv.at[peer])
-    o_prob[...] = (parts[0] + parts[1] + parts[2] + parts[3])[:1]
+    prob_out[...] = (parts[0] + parts[1] + parts[2] + parts[3])[:1]
+    copy = pltpu.make_async_copy(prob_out, o_prob, l_sem.at[1])
+    copy.start()
+    written.append(copy)
+    finish(nf - 1)
 
     for copy in (*sent, *x_sent, *t1.values(), *t2.values()):
         copy.wait_send()
@@ -502,18 +523,16 @@
     any_spec = pl.BlockSpec(memory_space=pl.ANY)
     vmem, dma = pltpu.VMEM, pltpu.SemaphoreType.DMA
     spec = pl.BlockSpec(memory_space=pltpu.VMEM)
-    grad = jax.ShapeDtypeStruct((ff, quarter), F32)
     two = 2 * quarter
-    outs = pl.pallas_call(
+    row_outs, prob_out, grads = pl.pallas_call(
         kernel,
         out_shape=(
-            jax.ShapeDtypeStruct((toks, quarter), BF16),
-            jax.ShapeDtypeStruct((toks, quarter), BF16),
+            jax.ShapeDtypeStruct((2, toks, quarter), BF16),
             jax.ShapeDtypeStruct((1, toks), F32),
-            grad, grad, grad,
+            jax.ShapeDtypeStruct((3, ff, quarter), F32),
         ),
         in_specs=[spec] * 4 + [any_spec] * 3,
-        out_specs=(spec,) * 3 + (any_spec,) * 3,
+        out_specs=(any_spec, any_spec, any_spec),
         scratch_shapes=[
             vmem((4, 3, ff, quarter), BF16),
             vmem((slots, two), BF16),
@@ -536,10 +555,12 @@
             vmem((toks, slots), BF16),
             vmem((toks, quarter), F32),
             vmem((4, 8, toks), F32),
+            vmem((2, toks, quarter), BF16),
+            vmem((1, toks), F32),
             dma((2, nf, 4)), dma((nf, 4)), dma((nf, 4)), dma((2, nf, 4)),
             dma, dma((pieces,)), dma((5,)), dma((3, pieces)), dma((4, pieces)),
             dma((2, pieces)), dma((2, pieces)), dma((pieces,)), dma((pieces,)),
-            dma, dma, dma((3,)), dma((4,)), dma((3, nf)), pltpu.SemaphoreType.REGULAR((2,)),
+            dma, dma, dma((3,)), dma((4,)), dma((nf,)), pltpu.SemaphoreType.REGULAR((2,)),
         ],
         compiler_params=pltpu.CompilerParams(
             collective_id=0, has_side_effects=True, vmem_limit_bytes=63000 * 1024
@@ -548,7 +569,7 @@
         tokens, cotangent, expert_ids.reshape(1, toks), route_prob.reshape(1, toks),
         gate_weight.T, up_weight.T, down_weight.T,
     )
-    return outs[0], outs[1], outs[2].reshape(toks), outs[3].T, outs[4].T, outs[5].T
+    return row_outs[0], row_outs[1], prob_out.reshape(toks), grads[0].T, grads[1].T, grads[2].T
 
 
 def solution(mesh):

time: 141 us -> 134 us (0.950)
  Pallas kernels: 133 us -> 128 us
  local copies, waits for them, and re-layouts: 6.97 us -> 4.97 us
    unnamed x14 -> x3, local copies, waits for them, and re-layouts: 6.97 us -> 0.52 us
    pallas_call x1, Pallas kernels: 133 us -> 128 us  [shards(): pl.pallas_call(kernel, out_shape=(jax.ShapeDtypeStruct((2, toks, quarter)...]
    transpose x0 -> x1, local copies, waits for them, and re-layouts: none -> 2.92 us  [shards(): grads[2]]
    squeeze x0 -> x1, local copies, waits for them, and re-layouts: none -> 1.53 us  [shards(): row_outs[1]]
where the time goes in v3:
time: 134 us
  Pallas kernels  128 us (96%)
  local copies, waits for them, and re-layouts  4.97 us (4%)
    pallas_call x1, Pallas kernels, shards(): pl.pallas_call(kernel, out_shape=(jax.ShapeDtypeStruct((2, toks, quarter)...  128 us
    transpose x1, local copies, waits for them, and re-layouts, shards(): grads[2]  2.92 us

profile of v3, /device:TPU:1, one launch (start us, length us, event | category | flops | bytes accessed | tf_op | source)
XLA Modules:
  0.0 133.6 jit_solution(553426455830849736)
XLA Ops:
  0.6 128.0 %shard_map.118 = (bf16[2,128,256]{2,1,0:T(8,128)(2,1)}, f32[1,128]{1,0:T(1,128)}, f32[3,704,256]{2,1,0:T(8,128)}) custom-call(bf16[128,1024]{1,0:T(8,128)(2,1)} %tok.1, bf16[128,1024]{1,0:T(8,128)(2,1)} %cot.1, s32[1,128]{1,0:T(1,128)} %bitcast.25, f32[1,128]{1,0:T(1,128)} %bitcast.26, bf16[704,256]{1,0:T(8,128)(2,1)} %bitcast.22, ...), custom_call_target="tpu_custom_call" | custom-call | tf_op jit(solution)/shard_map/pallas_call | solution.py:527
  128.6 1.5 %slice_bitcast_fusion.3 = (bf16[128,256]{1,0:T(8,128)(2,1)}, bf16[128,256]{1,0:T(8,128)(2,1)}) fusion(bf16[2,128,256]{2,1,0:T(8,128)(2,1)} %get-tuple-element.9), kind=kLoop, calls=%fused_computation.3 | loop fusion | bytes 262144 | tf_op jit(solution)/shard_map/squeeze | solution.py:572
  130.2 0.0 copy-start
  130.2 2.9 %slice_bitcast_fusion = (f32[256,704]{0,1:T(8,128)}, f32[256,704]{0,1:T(8,128)}, f32[256,704]{0,1:T(8,128)}) fusion(f32[3,704,256]{2,1,0:T(8,128)} %get-tuple-element.11), kind=kLoop, calls=%fused_computation | loop fusion | bytes 4325376 | tf_op jit(solution)/shard_map/transpose | solution.py:572
  133.1 0.0 copy-done
  133.1 0.5 copy.14
Async XLA Ops:
  130.2 2.9 %copy-start = (f32[1,128]{1,0:T(1,128)S(1)}, f32[1,128]{1,0:T(1,128)}, u32[]{:S(2)}) copy-start(f32[1,128]{1,0:T(1,128)} %get-tuple-element.10) | copy-start | bytes 1540

commit v4 on v3

--- a/solution.py
+++ b/solution.py
@@ -434,12 +434,13 @@
 
     relay_a(2, 0)
     relay_b(1)
-    relay_a(2, 1)
     for turn in back_turns:
         if turn == back_turns[-1]:
             relay_b(2)
             relay_a(3, 0)
         send_back(turn)
+        if turn == back_turns[0]:
+            relay_a(2, 1)
     relay_a(3, 1)
     relay_b(nf - 1)
 

time: 134 us -> 134 us (level)
  no operation moved by 1% of the time
where the time goes in v4:
time: 134 us
  Pallas kernels  128 us (96%)
  local copies, waits for them, and re-layouts  4.97 us (4%)
    pallas_call x1, Pallas kernels, shards(): pl.pallas_call(kernel, out_shape=(jax.ShapeDtypeStruct((2, toks, quarter)...  128 us
    transpose x1, local copies, waits for them, and re-layouts, shards(): grads[2]  2.92 us

profile of v4, /device:TPU:1, one launch (start us, length us, event | category | flops | bytes accessed | tf_op | source)
XLA Modules:
  0.0 133.6 jit_solution(13078615771240052407)
XLA Ops:
  0.6 128.0 %shard_map.118 = (bf16[2,128,256]{2,1,0:T(8,128)(2,1)}, f32[1,128]{1,0:T(1,128)}, f32[3,704,256]{2,1,0:T(8,128)}) custom-call(bf16[128,1024]{1,0:T(8,128)(2,1)} %tok.1, bf16[128,1024]{1,0:T(8,128)(2,1)} %cot.1, s32[1,128]{1,0:T(1,128)} %bitcast.25, f32[1,128]{1,0:T(1,128)} %bitcast.26, bf16[704,256]{1,0:T(8,128)(2,1)} %bitcast.22, ...), custom_call_target="tpu_custom_call" | custom-call | tf_op jit(solution)/shard_map/pallas_call | solution.py:528
  128.6 1.5 %slice_bitcast_fusion.3 = (bf16[128,256]{1,0:T(8,128)(2,1)}, bf16[128,256]{1,0:T(8,128)(2,1)}) fusion(bf16[2,128,256]{2,1,0:T(8,128)(2,1)} %get-tuple-element.9), kind=kLoop, calls=%fused_computation.3 | loop fusion | bytes 262144 | tf_op jit(solution)/shard_map/squeeze | solution.py:573
  130.2 0.0 copy-start
  130.2 2.9 %slice_bitcast_fusion = (f32[256,704]{0,1:T(8,128)}, f32[256,704]{0,1:T(8,128)}, f32[256,704]{0,1:T(8,128)}) fusion(f32[3,704,256]{2,1,0:T(8,128)} %get-tuple-element.11), kind=kLoop, calls=%fused_computation | loop fusion | bytes 4325376 | tf_op jit(solution)/shard_map/transpose | solution.py:573
  133.1 0.0 copy-done
  133.1 0.5 copy.14
Async XLA Ops:
  130.2 2.9 %copy-start = (f32[1,128]{1,0:T(1,128)S(1)}, f32[1,128]{1,0:T(1,128)}, u32[]{:S(2)}) copy-start(f32[1,128]{1,0:T(1,128)} %get-tuple-element.10) | copy-start | bytes 1540
